TPU v7x, 256 devices: a whole 4x4x8 slice. The times are simulated.
256 devices in a mesh: seq: 16 (over x, y_lo, core), ch: 16 (over z, y_hi).
Axes of the slice: x: 4, y: 4 (y_hi: 2, y_lo: 2; y = y_hi * 2 + y_lo), z: 8, core: 2. Of those that a mesh axis runs over, the one named last changes fastest.
Arguments:
- grad_out: bfloat16 [2048, 8192], P('seq', 'ch'), may hold values from -6 to 6
- out_weight: bfloat16 [8192, 8192], P('ch'), may hold values from -0.0625 to 0.0625
- query_gate: bfloat16 [2048, 8192], P('seq', 'ch'), may hold values from -6 to 6
- key_branch: bfloat16 [2048, 8192], P('seq', 'ch'), may hold values from -6 to 6
- value_branch: bfloat16 [2048, 8192], P('seq', 'ch'), may hold values from -6 to 6
- filter_taps: bfloat16 [2048, 8192], P('seq', 'ch'), may hold values from -4 to 4
Outputs:
- key_grad: bfloat16 [2048, 8192], P('seq', 'ch')
- value_grad: bfloat16 [2048, 8192], P('seq', 'ch')
- filter_grad: float32 [2048, 8192], P('seq', 'ch')
All inputs are finite; a program needn't handle non-finite values.
Results may differ from a plain program's by a relative error of at most 0.017.
Values may be sent and summed in bfloat16 or wider, within the bound.
A program may use at most 192 MiB of HBM per device.

v0:
```python
import math

import jax
import jax.numpy as jnp
from jax import lax
from jax.sharding import PartitionSpec as P


def build_tables(seg_len):
    twice_length = 2 * seg_len
    freq_index = jnp.arange(twice_length, dtype=jnp.int32)
    row_index = jnp.arange(seg_len, dtype=jnp.int32)
    angle_unit = 2.0 * math.pi / twice_length
    fwd_phase = (freq_index[:, None] * row_index[None, :] % twice_length).astype(
        jnp.float32
    ) * angle_unit
    back_phase = (freq_index[None, :] * (seg_len - row_index[:, None]) % twice_length).astype(
        jnp.float32
    ) * angle_unit
    window_pos = (freq_index + seg_len) % twice_length
    window_phase = (freq_index[None, :] * window_pos[:, None] % twice_length).astype(
        jnp.float32
    ) * angle_unit
    parity = jnp.where(freq_index % 2 == 0, 1.0, -1.0).astype(jnp.float32)[:, None]
    return (
        jnp.cos(fwd_phase).astype(jnp.bfloat16),
        jnp.sin(fwd_phase).astype(jnp.bfloat16),
        jnp.cos(back_phase).astype(jnp.bfloat16),
        jnp.sin(back_phase).astype(jnp.bfloat16),
        jnp.cos(window_phase).astype(jnp.bfloat16),
        jnp.sin(window_phase).astype(jnp.bfloat16),
        parity,
    )


def spectra(block_list, cosine_forward, sine_forward):
    cosine_piece = jnp.einsum(
        "qk,rkb->rqb", cosine_forward, block_list, preferred_element_type=jnp.float32
    )
    sine_piece = jnp.einsum(
        "qk,rkb->rqb", sine_forward, block_list, preferred_element_type=jnp.float32
    )
    return (cosine_piece, sine_piece)


def shards(grad_out, out_weight, query_gate, key_branch, value_branch, filter_taps):
    seg_len = query_gate.shape[0]
    channels = query_gate.shape[1]
    twice_length = 2 * seg_len
    segments = lax.axis_size("seq")
    my_index = lax.axis_index("seq")
    factor = 1.0 / math.sqrt(seg_len * segments)
    grad_mix = lax.dot_general(
        lax.all_gather(grad_out, "ch", axis=1, tiled=True),
        out_weight,
        (((1,), (1,)), ((), ())),
        preferred_element_type=jnp.float32,
    )
    gated_grad = (grad_mix * query_gate.astype(jnp.float32)).astype(jnp.bfloat16)
    conv_input = (key_branch.astype(jnp.float32) * value_branch.astype(jnp.float32)).astype(
        jnp.bfloat16
    )
    tables = build_tables(seg_len)
    (
        cosine_forward,
        sine_forward,
        cosine_backward,
        sine_backward,
        cosine_window,
        sine_window,
        parity,
    ) = tables
    all_taps = lax.all_gather(filter_taps, "seq", axis=0, tiled=True)
    tap_cos, tap_sin = spectra(
        all_taps.reshape(segments, seg_len, channels), cosine_forward, sine_forward
    )
    kern_cos = jnp.concatenate([jnp.zeros_like(tap_cos[:1]), tap_cos[:-1]], 0) + parity * tap_cos
    kern_sin = jnp.concatenate([jnp.zeros_like(tap_sin[:1]), tap_sin[:-1]], 0) + parity * tap_sin
    own_cos, own_sin = spectra(conv_input[None], cosine_forward, sine_forward)
    own_cos = own_cos[0]
    own_sin = own_sin[0]
    zero_spec = jnp.zeros((twice_length, channels), jnp.float32)
    initial = (zero_spec, zero_spec, jnp.zeros(((segments + 1) * seg_len, channels), jnp.float32))
    piece_data = lax.all_gather(gated_grad, "seq", axis=0, tiled=True)
    block_count = piece_data.shape[0] // seg_len
    seg_ids = jnp.arange(block_count, dtype=jnp.int32)
    block_list = piece_data.reshape(block_count, seg_len, channels)
    grad_cos, grad_sin = spectra(block_list, cosine_forward, sine_forward)
    lag_steps = seg_ids - my_index
    inside = seg_ids < segments
    live_mask = ((lag_steps >= 0) & inside).astype(jnp.float32)[:, None, None]
    lag_clip = jnp.clip(lag_steps, 0, segments - 1)
    lag_kcos = jnp.take(kern_cos, lag_clip, axis=0)
    lag_ksin = jnp.take(kern_sin, lag_clip, axis=0)
    running_real = jnp.sum(live_mask * (grad_cos * lag_kcos + grad_sin * lag_ksin), axis=0)
    running_imaginary = jnp.sum(live_mask * (grad_sin * lag_kcos - grad_cos * lag_ksin), axis=0)
    product_real = (own_cos * grad_cos + own_sin * grad_sin).astype(jnp.bfloat16)
    product_imaginary = (own_sin * grad_cos - own_cos * grad_sin).astype(jnp.bfloat16)
    windows = jnp.einsum(
        "an,hny->hay", cosine_window, product_real, preferred_element_type=jnp.float32
    ) - jnp.einsum(
        "an,hny->hay", sine_window, product_imaginary, preferred_element_type=jnp.float32
    )
    windows = windows * (live_mask / twice_length)

    def place(item_index, buffer):
        offset = lag_clip[item_index] * seg_len
        current = lax.dynamic_slice_in_dim(buffer, offset, twice_length, 0)
        return lax.dynamic_update_slice_in_dim(buffer, current + windows[item_index], offset, 0)

    buffer = lax.fori_loop(0, block_list.shape[0], place, initial[2])
    convolution_gradient = (
        jnp.dot(
            cosine_backward, running_real.astype(jnp.bfloat16), preferred_element_type=jnp.float32
        )
        - jnp.dot(
            sine_backward,
            running_imaginary.astype(jnp.bfloat16),
            preferred_element_type=jnp.float32,
        )
    ) / twice_length
    own_rows = lax.psum_scatter(
        buffer[seg_len:].astype(jnp.bfloat16), "seq", scatter_dimension=0, tiled=True
    ).astype(jnp.float32)
    filter_grad = own_rows * factor
    key_grad = (convolution_gradient * value_branch.astype(jnp.float32)).astype(jnp.bfloat16)
    value_grad = (convolution_gradient * key_branch.astype(jnp.float32)).astype(jnp.bfloat16)
    return (key_grad, value_grad, filter_grad)


def solution(mesh):
    return jax.shard_map(
        shards,
        mesh=mesh,
        in_specs=(
            P("seq", "ch"),
            P("ch", None),
            P("seq", "ch"),
            P("seq", "ch"),
            P("seq", "ch"),
            P("seq", "ch"),
        ),
        out_specs=(P("seq", "ch"), P("seq", "ch"), P("seq", "ch")),
        check_vma=False,
    )
```

profile of v0, /device:TPU:1, one launch (start us, length us, event | category | flops | bytes accessed | tf_op | source)
XLA Modules:
  0.0 389.5 jit_solution(9335437715561925159)
XLA Ops:
  8.7 85.9 %all-gather.4.cloned.1.call-done = bf16[128,8192]{1,0:T(8,128)(2,1)} async-done(((bf16[128,512]{1,0:T(8,128)(2,1)}), bf16[128,8192]{1,0:T(8,128)(2,1)}) %all-gather.4.cloned.1.call-update) | async-done | bytes 2097168 | tf_op jit(solution)/shard_map/all_gather | solution.py:54
  94.6 7.6 %fusion.22 = bf16[128,512]{1,0:T(8,128)(2,1)} fusion(bf16[128,8192]{1,0:T(8,128)(2,1)} %all-gather.4.cloned.1.call-done, bf16[512,8192]{1,0:T(8,128)(2,1)} %param.11, bf16[128,512]{1,0:T(8,128)(2,1)} %param.12), kind=kOutput, calls=%fused_computation.40 | convolution fusion | flops 1073938432 | bytes 10747904 | tf_op jit(solution)/shard_map/dot_general | solution.py:53
  103.8 30.2 %all-gather.8.cloned.1.call-done = bf16[2048,512]{1,0:T(8,128)(2,1)} async-done(((bf16[128,512]{1,0:T(8,128)(2,1)}), bf16[2048,512]{1,0:T(8,128)(2,1)}) %all-gather.8.cloned.1.call-update) | async-done | bytes 2097168 | tf_op jit(solution)/shard_map/all_gather | solution.py:73
  134.0 3.2 convolution_bitcast_fusion.1
  137.3 4.5 %slice.17 = f32[15,256,512]{2,1,0:T(8,128)} slice(f32[16,256,512]{2,1,0:T(8,128)S(1)} %convolution_bitcast_fusion.1), slice={[0:15], [0:256], [0:512]} | slice | bytes 15728640 | tf_op jit(solution)/shard_map/slice | solution.py:77
  143.5 3.2 copy-done.1
  146.8 4.6 %slice.18 = f32[15,256,512]{2,1,0:T(8,128)} slice(f32[16,256,512]{2,1,0:T(8,128)S(1)} %convolution_bitcast_fusion), slice={[0:15], [0:256], [0:512]} | slice | bytes 15728640 | tf_op jit(solution)/shard_map/slice | solution.py:78
  151.4 19.0 %multiply_add_fusion.1 = (f32[16,256,512]{2,1,0:T(8,128)}, f32[16,256,512]{2,1,0:T(8,128)}) fusion(f32[16,256,512]{2,1,0:T(8,128)} %copy-done, f32[15,256,512]{2,1,0:T(8,128)} %slice.17, f32[256]{0:T(256)S(1)} %compare_select_fusion.3, f32[16,256,512]{2,1,0:T(8,128)} %copy-done.1, f32[15,256,512]{2,1,0:T(8,128)} %slice.18), kind=kLoop, calls=%fused_computation.25 | loop fusion | flops 8388608 | bytes 49284096 | tf_op jit(solution)/shard_map/add | solution.py:77
  170.4 7.7 %gather_fusion = f32[16,256,512]{2,1,0:T(8,128)} fusion(f32[16,256,512]{2,1,0:T(8,128)} %get-tuple-element.108, s32[1024]{0:T(1024)S(1)} %pad_clamp_fusion), kind=kCustom, calls=%fused_computation.clone | custom fusion | bytes 16777280 | tf_op jit(solution)/shard_map/jit(_take)/gather | solution.py:93
  178.1 9.2 %copy.18 = f32[16,256,512]{1,2,0:T(8,128)} copy(f32[16,256,512]{2,1,0:T(8,128)} %gather_fusion) | data formatting | bytes 16777216 | tf_op jit(solution)/shard_map/jit(_take)/gather | solution.py:93
  187.3 7.7 %gather_fusion.1 = f32[16,256,512]{2,1,0:T(8,128)} fusion(f32[16,256,512]{2,1,0:T(8,128)} %get-tuple-element.109, s32[1024]{0:T(1024)S(1)} %pad_clamp_fusion), kind=kCustom, calls=%fused_computation.1.clone | custom fusion | bytes 16777280 | tf_op jit(solution)/shard_map/jit(_take)/gather | solution.py:94
  195.0 9.3 %copy.20 = f32[16,256,512]{1,2,0:T(8,128)} copy(f32[16,256,512]{2,1,0:T(8,128)} %gather_fusion.1) | data formatting | bytes 16777216 | tf_op jit(solution)/shard_map/jit(_take)/gather | solution.py:94
  204.3 3.5 fusion.57
  207.7 10.9 %fusion.6 = (bf16[256,512]{0,1:T(8,128)(2,1)S(1)}, bf16[256,512]{0,1:T(8,128)(2,1)S(1)}, f32[16,512,256]{2,1,0:T(8,128)}) fusion(f32[16,512,256]{2,1,0:T(8,128)S(1)} %fusion.57, f32[16,256,512]{1,2,0:T(8,128)} %copy.20, f32[16,256,512]{1,2,0:T(8,128)} %copy.18, f32[16]{0:T(128)S(1)} %get-tuple-element.114, pred[16]{0:T(512)(128)(4,1)S(1)} %get-tuple-element.113, ...), kind=kOutput, calls=%fused_computation.14 | convolution fusion | flops 562266112 | bytes 36175952 | tf_op jit(solution)/shard_map/qk,rkb->rqb/dot_general | solution.py:40
  218.6 9.5 %fusion.11 = f32[16,512,256]{2,1,0:T(8,128)} fusion(f32[16,512,256]{2,1,0:T(8,128)} %get-tuple-element.110, f32[16,512,256]{2,1,0:T(8,128)S(1)} %fusion.57, f32[256,512]{0,1:T(8,128)S(1)} %convolution_bitcast_fusion.2, f32[256,512]{0,1:T(8,128)S(1)} %convolution_bitcast_fusion.3, s32[256]{0:T(256)S(1)} %and_select_fusion), kind=kOutput, calls=%fused_computation.26 | convolution fusion | flops 1083113472 | bytes 26215424 | tf_op jit(solution)/shard_map/an,hny->hay/dot_general | solution.py:101
  228.1 11.8 %multiply_bitcast_fusion = f32[16,256,512]{1,2,0:T(8,128)} fusion(f32[16,512,256]{2,1,0:T(8,128)} %fusion.11, f32[16]{0:T(128)S(1)} %broadcast_select_fusion, f32[16,512,256]{2,1,0:T(8,128)} %get-tuple-element.110, f32[16,512,256]{2,1,0:T(8,128)S(1)} %fusion.57, f32[256,512]{0,1:T(8,128)S(1)} %convolution_bitcast_fusion.2, ...), kind=kOutput, calls=%fused_computation.23 | convolution fusion | flops 1087307776 | bytes 34604096 | tf_op jit(solution)/shard_map/an,hny->hay/dot_general | solution.py:99
  239.9 2.6 broadcast_in_dim.30
  242.5 71.4 %while.13 = (s32[]{:T(128)}, f32[2176,512]{1,0:T(8,128)}, s32[16]{0:T(128)S(1)}, f32[16,256,512]{1,2,0:T(8,128)}, s32[]{:T(128)}, /*index=5*/s32[1]{0:T(128)}, s32[]{:T(128)}, s32[]{:T(128)}) while((s32[]{:T(128)}, f32[2176,512]{1,0:T(8,128)}, s32[16]{0:T(128)S(1)}, f32[16,256,512]{1,2,0:T(8,128)}, s32[]{:T(128)}, /*index=5*/s32[1]{0:T(128)}, ...), condition=%wide.region_3.5_spmd, body=%wide.region_2.4_spmd.sunk | while | flops 131078 | bytes 3670167 | solution.py:111
  262.9 1.9 fusion.115
  267.3 2.0 fusion.115
  294.1 1.9 fusion.115
  307.5 1.9 fusion.115
  313.9 3.8 slice.21
  319.8 61.5 %reduce-scatter.2.cloned.1.call-done = bf16[128,512]{1,0:T(8,128)(2,1)} async-done(((bf16[2048,512]{1,0:T(8,128)(2,1)}), bf16[128,512]{1,0:T(8,128)(2,1)}) %reduce-scatter.2.cloned.1.call-update) | async-done | bytes 131088 | tf_op jit(solution)/shard_map/reduce_scatter | solution.py:122
  (93 shorter events, 61.3 us)
Async XLA Ops:
  7.2 95.2 %copy-start.4 = (bf16[128,512]{1,0:T(8,128)(2,1)S(1)}, bf16[128,512]{1,0:T(8,128)(2,1)}, u32[]{:S(2)}) copy-start(bf16[128,512]{1,0:T(8,128)(2,1)} %param.13) | copy-start | bytes 393220
  7.2 95.2 %copy-start.5 = (bf16[128,512]{1,0:T(8,128)(2,1)S(1)}, bf16[128,512]{1,0:T(8,128)(2,1)}, u32[]{:S(2)}) copy-start(bf16[128,512]{1,0:T(8,128)(2,1)} %param.14) | copy-start | bytes 393220
  7.2 87.4 %all-gather.4.cloned.1.call-start = ((), (), s32[]{:S(2)}) async-start(), calls=%async_computation.1 | async-start | bytes 2228224 | tf_op jit(solution)/shard_map/all_gather | solution.py:54
  7.9 126.1 %all-gather.8.cloned.1.call-start = ((), (), s32[]{:S(2)}) async-start(), calls=%async_computation.3 | async-start | bytes 2228224 | tf_op jit(solution)/shard_map/all_gather | solution.py:73
  8.7 195.6 %all-gather.6.cloned.1.call-start = ((), (), s32[]{:S(2)}) async-start(), calls=%async_computation.2 | async-start | bytes 2228224 | tf_op jit(solution)/shard_map/all_gather | solution.py:84
  102.2 279.1 %reduce-scatter.2.cloned.1.call-start = ((), (), s32[]{:S(2)}) async-start(), calls=%async_computation.4 | async-start | bytes 2228224 | tf_op jit(solution)/shard_map/reduce_scatter | solution.py:122
  137.3 6.2 %copy-start = (f32[16,256,512]{2,1,0:T(8,128)}, f32[16,256,512]{2,1,0:T(8,128)S(1)}, u32[]{:S(2)}) copy-start(f32[16,256,512]{2,1,0:T(8,128)S(1)} %convolution_bitcast_fusion.1) | copy-start | bytes 25165828
  137.3 4.6 %copy-start.2 = (bf16[2048,512]{1,0:T(8,128)(2,1)S(1)}, bf16[2048,512]{1,0:T(8,128)(2,1)}, u32[]{:S(2)}) copy-start(bf16[2048,512]{1,0:T(8,128)(2,1)} %all-gather.8.cloned.1.call-done) | copy-start | bytes 6291460
  143.5 3.2 copy-start.1
  204.3 3.5 copy-start.3
Sparse Core Ops, SparseCore 0:
  10.5 84.1 all-gather.3
  96.5 37.5 all-gather.7
  136.5 36.3 all-gather.5
  317.9 63.4 reduce-scatter.1
where the time goes:
time: 394 us; the launch traced here: 390 us
  waiting for transfers between devices  179 us (45%)
  local copies, waits for them, and re-layouts  82.5 us (21%)
  matrix products  51.6 us (13%)
  other arithmetic  51.6 us (13%)
  between operations  13.9 us (4%)
  loops' own time  10.7 us (3%)
    all_gather x1, waiting for transfers between devices, shards(): lax.all_gather(grad_out, 'ch', axis=1, tiled=True)  85.9 us
    reduce_scatter x1, waiting for transfers between devices, shards(): lax.psum_scatter(buffer[seg_len:].astype(jnp.bfloat16), 'seq', scatter_di...  61.5 us
    dynamic_update_slice x16, other arithmetic, place(): lax.dynamic_update_slice_in_dim(buffer, current + windows[item_index], of...  30.9 us
    all_gather x1, waiting for transfers between devices, shards(): all_taps = lax.all_gather(filter_taps, 'seq', axis=0, tiled=True)  30.2 us
    dynamic_slice x32, local copies, waits for them, and re-layouts, place(): windows[item_index]  20.5 us
    add x1, other arithmetic, shards(): jnp.concatenate([jnp.zeros_like(tap_cos[:1]), tap_cos[:-1]], 0)  19 us
    gather x2, local copies, waits for them, and re-layouts, shards(): lag_ksin = jnp.take(kern_sin, lag_clip, axis=0)  16.9 us
    gather x2, local copies, waits for them, and re-layouts, shards(): lag_kcos = jnp.take(kern_cos, lag_clip, axis=0)  16.9 us
  transfers between devices with their start and end apart: 4, of which 3 were waited for; matrix products, arithmetic and copies ran while one was open for 20% of the time, Pallas kernels for 0%

commit v1 on v0

v1 whole, which is shorter than its diff:
```python
import functools
import math

import jax
import jax.numpy as jnp
import numpy as np
from jax import lax
from jax.experimental import pallas as pl
from jax.experimental.pallas import tpu as pltpu
from jax.sharding import PartitionSpec as P

F32 = jnp.float32
BF16 = jnp.bfloat16
MESH = pl.DeviceIdType.MESH

N_SEQ = 16
N_CH = 16
NZ = 8
LS = 128
CH = 512
SUB = CH // N_SEQ
SEG = 256
NSEG = LS * N_SEQ // SEG


def tables():
    m = 2 * SEG
    t = np.arange(SEG)
    theta = 2.0 * np.pi * ((t[:, None] * t[None, :]) % m) / m
    fwd = np.concatenate([np.cos(theta), np.sin(theta)], 1)
    fwd[:, SEG] = np.where(t % 2 == 0, 1.0, -1.0)
    weight = np.full((m, 1), 2.0 / m)
    weight[0] = weight[SEG] = 1.0 / m
    return jnp.asarray(fwd, BF16), jnp.asarray(weight * fwd.T, BF16)


Z_OFF = (0, -1, -2, -3, 1, 2, 3, 4)
PLUS = (0, 1, 2, 3, 7)
MINUS = (0, 4, 5, 6, 7)
HALF = LS // 2


def kernel(
    go_hbm, w_hbm, q_hbm, key_hbm, val_hbm, taps_hbm, fwd_hbm, inv_hbm,
    kg_ref, vg_ref, fg_ref,
    x_v, w_v, q_v, key_v, val_v, taps_v, fwd_v, inv_v, acc,
    ct_s, tt_s, gt_s, qt, c_r, t_r, g_r, gsp, ksp, csp, abuf, y_s, l_s, y_r, l_r,
    in_sem, w_sem, ring_send, ring_recv, a2a_send, a2a_recv,
):
    s = lax.axis_index("seq")
    c = lax.axis_index("ch")
    z = c // 2
    h = c % 2

    def ch_of(zz, hh):
        return lax.rem(zz + 2 * NZ, NZ) * 2 + hh

    up = ch_of(z + 1, h)
    down = ch_of(z - 1, h)
    across = z * 2 + (1 - h)

    barrier = pltpu.get_barrier_semaphore()
    for peer in (up, down, across):
        pl.semaphore_signal(barrier, inc=1, device_id={"ch": peer}, device_id_type=MESH)
    for k in range(1, N_SEQ):
        pl.semaphore_signal(
            barrier, inc=1, device_id={"seq": lax.rem(s + k, N_SEQ)}, device_id_type=MESH
        )

    loads = []
    for i, (src, dst) in enumerate((
        (key_hbm, key_v), (val_hbm, val_v), (taps_hbm, taps_v), (q_hbm, q_v),
        (go_hbm, x_v.at[0]), (fwd_hbm, fwd_v), (inv_hbm, inv_v),
    )):
        copy = pltpu.make_async_copy(src, dst, in_sem.at[i])
        copy.start()
        loads.append(copy)
    w_loads = []
    for slot in range(N_CH):
        own = slot < NZ
        chunk = ch_of(z + Z_OFF[slot % NZ], h if own else 1 - h)
        copy = pltpu.make_async_copy(
            w_hbm.at[:, pl.ds(pl.multiple_of(chunk * CH, CH), CH)], w_v.at[slot], w_sem.at[slot]
        )
        w_loads.append(copy)
    order = (0, 1, 4, 8, 2, 5, 9, 12, 3, 6, 10, 13, 7, 11, 14, 15)
    for slot in order:
        w_loads[slot].start()

    loads[0].wait()
    loads[1].wait()
    ct_s[...] = (key_v[...].astype(F32) * val_v[...].astype(F32)).T.astype(BF16)
    loads[2].wait()
    tt_s[...] = taps_v[...].astype(F32).T.astype(BF16)
    loads[4].wait()

    pl.semaphore_wait(barrier, 3 + N_SEQ - 1)

    rows = (pl.ds(0, HALF), pl.ds(HALF, HALF))
    sent = []

    def push(src, dst, half, to):
        copy = pltpu.make_async_remote_copy(
            src_ref=x_v.at[src, rows[half]],
            dst_ref=x_v.at[dst, rows[half]],
            send_sem=ring_send.at[len(sent)],
            recv_sem=ring_recv.at[dst, half],
            device_id={"ch": to},
            device_id_type=MESH,
        )
        copy.start()
        sent.append(copy)

    def arrived(slot, half):
        pltpu.make_async_remote_copy(
            src_ref=x_v.at[slot, rows[half]],
            dst_ref=x_v.at[slot, rows[half]],
            send_sem=ring_send.at[0],
            recv_sem=ring_recv.at[slot, half],
            device_id={"ch": up},
            device_id_type=MESH,
        ).wait_recv()

    def mult(slot):
        w_loads[slot].wait()
        part = lax.dot_general(
            w_v[slot], x_v[slot], (((1,), (1,)), ((), ())), preferred_element_type=F32
        )
        if slot == 0:
            acc[...] = part
        else:
            acc[...] += part

    def forward(step, base):
        if step < 4:
            for chain, to, last in ((PLUS, up, 0), (MINUS, down, 1)):
                for half in (0, 1):
                    arrived(base + chain[step], half)
                    if step < 3 or half == last:
                        push(base + chain[step], base + chain[step + 1], half, to)
        else:
            arrived(base + PLUS[4], 0)
            arrived(base + PLUS[4], 1)

    for half in (0, 1):
        push(0, PLUS[1], half, up)
        push(0, MINUS[1], half, down)
    for half in (0, 1):
        push(0, NZ, half, across)

    def scatter(block, recv, which):
        my_row = pl.ds(pl.multiple_of((s // 2) * SUB, SUB), SUB)
        my_col = pl.ds(pl.multiple_of((s % 2) * LS, LS), LS)
        pltpu.make_async_copy(
            block.at[pl.ds(pl.multiple_of(s * SUB, SUB), SUB)],
            recv.at[my_row, my_col],
            a2a_recv.at[which],
        ).start()
        for k in range(1, N_SEQ):
            to = lax.rem(s + k, N_SEQ)
            pltpu.make_async_remote_copy(
                src_ref=block.at[pl.ds(pl.multiple_of(to * SUB, SUB), SUB)],
                dst_ref=recv.at[my_row, my_col],
                send_sem=a2a_send.at[which],
                recv_sem=a2a_recv.at[which],
                device_id={"seq": to},
                device_id_type=MESH,
            ).start()

    def collect(block, recv, which):
        my_row = pl.ds(pl.multiple_of(s * SUB, SUB), SUB)

        def piece(i):
            return block.at[
                pl.ds(pl.multiple_of((i // 2) * SUB, SUB), SUB),
                pl.ds(pl.multiple_of((i % 2) * LS, LS), LS),
            ]

        pltpu.make_async_copy(piece(s), recv.at[my_row], a2a_recv.at[which]).start()
        for k in range(1, N_SEQ):
            to = lax.rem(s + k, N_SEQ)
            pltpu.make_async_remote_copy(
                src_ref=piece(to),
                dst_ref=recv.at[my_row],
                send_sem=a2a_send.at[which],
                recv_sem=a2a_recv.at[which],
                device_id={"seq": to},
                device_id_type=MESH,
            ).start()

    def all_in(recv, which):
        pltpu.make_async_copy(recv, recv, a2a_recv.at[which]).wait()

    def all_out(block, which):
        rows_sent = block.shape[0] - block.shape[0] // N_SEQ
        part = block.at[pl.ds(0, rows_sent)]
        pltpu.make_async_copy(part, part, a2a_send.at[which]).wait()

    scatter(ct_s, c_r, 0)
    scatter(tt_s, t_r, 1)

    loads[3].wait()
    qt[...] = q_v[...].astype(F32).T
    mult(0)

    sign = jnp.where(
        lax.broadcasted_iota(jnp.int32, (1, SEG), 1) % 2 == 0, 1.0, -1.0
    ).astype(F32)
    first = lax.broadcasted_iota(jnp.int32, (1, SEG), 1) == 0

    forward(1, 0)
    mult(1)
    mult(4)
    for half in (0, 1):
        arrived(NZ, half)
        push(NZ, NZ + PLUS[1], half, up)
        push(NZ, NZ + MINUS[1], half, down)
    mult(8)
    forward(2, 0)
    mult(2)
    mult(5)
    forward(1, NZ)
    mult(9)
    mult(12)
    forward(3, 0)

    def put3(ref, cos, sin):
        ref[:, pl.ds(0, SEG)] = cos
        ref[:, pl.ds(SEG, SEG)] = jnp.where(first, 0.0, sin)
        ref[:, pl.ds(2 * SEG, SEG)] = jnp.where(first, sin, cos)

    loads[5].wait()
    all_in(c_r, 0)
    spec = jnp.dot(c_r[...], fwd_v[...], preferred_element_type=F32)
    put3(csp, spec[:, :SEG], spec[:, SEG:])
    mult(3)
    mult(6)
    forward(2, NZ)
    all_in(t_r, 1)
    spec = jnp.dot(t_r[...], fwd_v[...], preferred_element_type=F32)
    before = jnp.concatenate([jnp.zeros((SUB, 2 * SEG), F32), spec[:-SUB]], 0)
    put3(
        ksp,
        spec[:, :SEG] + sign * before[:, :SEG],
        spec[:, SEG:] + sign * before[:, SEG:],
    )
    mult(10)
    mult(13)
    forward(4, 0)
    mult(7)
    forward(3, NZ)
    mult(11)
    mult(14)
    loads[6].wait()
    forward(4, NZ)
    mult(15)

    gt_s[...] = (acc[...] * qt[...]).astype(BF16)
    scatter(gt_s, g_r, 2)
    all_in(g_r, 2)
    gsp[...] = jnp.dot(g_r[...], fwd_v[...], preferred_element_type=F32)

    tile = 16
    cols = SEG // 128

    def at(ref, seg, row, part, col):
        return ref[
            pl.ds(pl.multiple_of(seg * SUB + row * tile, tile), tile),
            pl.ds(pl.multiple_of(part * SEG + col * 128, 128), 128),
        ]

    def put(seg, row, part, col, value):
        abuf[
            pl.ds(pl.multiple_of(seg * SUB + row * tile, tile), tile),
            pl.ds(pl.multiple_of(part * SEG + col * 128, 128), 128),
        ] = value.astype(BF16)

    def pair(ref, i, r, row, col):
        ga, gb = at(gsp, i, row, 0, col), at(gsp, i, row, 1, col)
        ka, kb, k2 = (at(ref, r, row, part, col) for part in range(3))
        return ga * ka + gb * kb, gb * k2 - ga * kb

    @pl.loop(0, (SUB // tile) * cols)
    def _(pos):
        row, col = pos // cols, pos % cols
        for j in range(NSEG):
            re = im = None
            for i in range(j, NSEG):
                a, b = pair(ksp, i, i - j, row, col)
                re, im = (a, b) if re is None else (re + a, im + b)
            put(j, row, 0, col, re)
            put(j, row, 1, col, im)

    y_s[...] = jnp.dot(abuf[...], inv_v[...], preferred_element_type=F32).astype(BF16)
    collect(y_s, y_r, 3)

    lane_sign = sign[:, :128]

    @pl.loop(0, (SUB // tile) * cols)
    def _(pos):
        row, col = pos // cols, pos % cols
        later = None
        for r in reversed(range(NSEG)):
            re = im = None
            for j in range(NSEG - r):
                a, b = pair(csp, j + r, j, row, col)
                re, im = (a, b) if re is None else (re + a, im + b)
            if later is None:
                put(r, row, 0, col, re)
                put(r, row, 1, col, im)
            else:
                put(r, row, 0, col, re + lane_sign * later[0])
                put(r, row, 1, col, im + lane_sign * later[1])
            later = (re, im)

    l_s[...] = jnp.dot(abuf[...], inv_v[...], preferred_element_type=F32).astype(BF16)
    collect(l_s, l_r, 4)

    all_in(y_r, 3)
    conv = y_r[...].astype(F32).T
    kg_ref[...] = (conv * val_v[...].astype(F32)).astype(BF16)
    vg_ref[...] = (conv * key_v[...].astype(F32)).astype(BF16)
    all_in(l_r, 4)
    fg_ref[...] = l_r[...].astype(F32).T * (1.0 / math.sqrt(LS * N_SEQ))

    for copy in sent:
        copy.wait_send()
    for which, block in enumerate((ct_s, tt_s, gt_s, y_s, l_s)):
        all_out(block, which)


def shards(grad_out, out_weight, query_gate, key_branch, value_branch, filter_taps):
    fwd, inv = tables()
    any_spec = pl.BlockSpec(memory_space=pl.ANY)
    vmem_spec = pl.BlockSpec(memory_space=pltpu.VMEM)
    block = (LS, CH)
    turned = (CH, LS)
    local = (NSEG * SUB, SEG)
    return pl.pallas_call(
        kernel,
        out_shape=(
            jax.ShapeDtypeStruct(block, BF16),
            jax.ShapeDtypeStruct(block, BF16),
            jax.ShapeDtypeStruct(block, F32),
        ),
        in_specs=[any_spec] * 8,
        out_specs=(vmem_spec,) * 3,
        scratch_shapes=[
            pltpu.VMEM((N_CH, LS, CH), BF16),
            pltpu.VMEM((N_CH, CH, CH), BF16),
            pltpu.VMEM(block, BF16),
            pltpu.VMEM(block, BF16),
            pltpu.VMEM(block, BF16),
            pltpu.VMEM(block, BF16),
            pltpu.VMEM((SEG, 2 * SEG), BF16),
            pltpu.VMEM((2 * SEG, SEG), BF16),
            pltpu.VMEM(turned, F32),
            pltpu.VMEM(turned, BF16),
            pltpu.VMEM(turned, BF16),
            pltpu.VMEM(turned, BF16),
            pltpu.VMEM(turned, F32),
            pltpu.VMEM(local, BF16),
            pltpu.VMEM(local, BF16),
            pltpu.VMEM(local, BF16),
            pltpu.VMEM((NSEG * SUB, 2 * SEG), F32),
            pltpu.VMEM((NSEG * SUB, 3 * SEG), F32),
            pltpu.VMEM((NSEG * SUB, 3 * SEG), F32),
            pltpu.VMEM((NSEG * SUB, 2 * SEG), BF16),
            pltpu.VMEM(local, BF16),
            pltpu.VMEM(local, BF16),
            pltpu.VMEM(turned, BF16),
            pltpu.VMEM(turned, BF16),
            pltpu.SemaphoreType.DMA((7,)),
            pltpu.SemaphoreType.DMA((N_CH,)),
            pltpu.SemaphoreType.DMA((30,)),
            pltpu.SemaphoreType.DMA((N_CH, 2)),
            pltpu.SemaphoreType.DMA((5,)),
            pltpu.SemaphoreType.DMA((5,)),
        ],
        compiler_params=pltpu.CompilerParams(
            collective_id=0, has_side_effects=True, vmem_limit_bytes=40 << 20
        ),
        name="hyena_backward",
    )(grad_out, out_weight, query_gate, key_branch, value_branch, filter_taps, fwd, inv)


def solution(mesh):
    spec = P("seq", "ch")
    return jax.shard_map(
        shards,
        mesh=mesh,
        in_specs=(spec, P("ch", None), spec, spec, spec, spec),
        out_specs=(spec, spec, spec),
        check_vma=False,
    )
```

time: 394 us -> 61.2 us (0.16); the launches traced: 390 us -> 60.9 us
  waiting for transfers between devices: 179 us -> 0 us
  local copies, waits for them, and re-layouts: 82.5 us -> 11.8 us
  matrix products: 51.6 us -> 0 us
  other arithmetic: 51.6 us -> 0 us
  Pallas kernels: 0 us -> 48.4 us
  between operations: 13.9 us -> 0.66 us
  loops' own time: 10.7 us -> 0 us
    all_gather x3 -> x0, waiting for transfers between devices: 116 us -> none  [the longest x1 85.9 us: shards(): lax.all_gather(grad_out, 'ch', axis=1, tiled=True)]
    reduce_scatter x1 -> x0, waiting for transfers between devices: 61.5 us -> none  [shards(): lax.psum_scatter(buffer[seg_len:].astype(jnp.bfloat16), 'seq', scatter_di...]
    dot_general x11 -> x0, matrix products: 51.6 us -> none  [the longest x3 13.3 us: spectra(): jnp.einsum('qk,rkb->rqb', sine_forward, block_list, preferred_element_typ...]
    pallas_call x0 -> x1, Pallas kernels: none -> 48.4 us  [shards(): pl.pallas_call(kernel, out_shape=(jax.ShapeDtypeStruct(block, BF16), jax....]
    gather x4 -> x0, local copies, waits for them, and re-layouts: 33.9 us -> none  [the longest x2 16.9 us: shards(): lag_ksin = jnp.take(kern_sin, lag_clip, axis=0)]
    dynamic_update_slice x16 -> x0, other arithmetic: 30.9 us -> none  [place(): lax.dynamic_update_slice_in_dim(buffer, current + windows[item_index], of...]
    dynamic_slice x48 -> x0, local copies, waits for them, and re-layouts: 29.8 us -> none  [the longest x32 20.5 us: place(): windows[item_index]]
    add x1 -> x0, other arithmetic: 19 us -> none  [shards(): jnp.concatenate([jnp.zeros_like(tap_cos[:1]), tap_cos[:-1]], 0)]
  transfers between devices with their start and end apart: 4 -> 0, of which waited for: 3 -> 0; matrix products, arithmetic and copies ran while one was open for 20% -> 0% of each run, Pallas kernels for 0% -> 0%
where the time goes in v1:
time: 61.2 us; the launch traced here: 60.9 us
  Pallas kernels  48.4 us (79%)
  local copies, waits for them, and re-layouts  11.8 us (19%)
  between operations  0.66 us (1%)
    pallas_call x1, Pallas kernels, shards(): pl.pallas_call(kernel, out_shape=(jax.ShapeDtypeStruct(block, BF16), jax....  48.4 us
    unnamed x19, local copies, waits for them, and re-layouts  11.8 us

profile of v1, /device:TPU:1, one launch (start us, length us, event | category | flops | bytes accessed | tf_op | source)
XLA Modules:
  0.0 60.9 jit_solution(5240865981275044132)
XLA Ops:
  0.6 0.0 copy-start
  0.6 3.4 %copy-done = bf16[512,8192]{1,0:T(8,128)(2,1)S(1)} copy-done((bf16[512,8192]{1,0:T(8,128)(2,1)S(1)}, bf16[512,8192]{1,0:T(8,128)(2,1)}, u32[]{:S(2)}) %copy-start) | copy-done | bytes 8388632
  4.0 0.0 copy-start.1
  4.0 0.9 %copy-done.1 = bf16[512,256]{1,0:T(8,128)(2,1)S(1)} copy-done((bf16[512,256]{1,0:T(8,128)(2,1)S(1)}, bf16[512,256]{1,0:T(8,128)(2,1)}, u32[]{:S(2)}) %copy-start.1) | copy-done | bytes 262168
  5.0 0.0 copy-start.2
  5.0 0.9 %copy-done.2 = bf16[256,512]{1,0:T(8,128)(2,1)S(1)} copy-done((bf16[256,512]{1,0:T(8,128)(2,1)S(1)}, bf16[256,512]{1,0:T(8,128)(2,1)}, u32[]{:S(2)}) %copy-start.2) | copy-done | bytes 262168
  5.9 0.0 copy-start.3
  5.9 0.9 %copy-done.3 = bf16[128,512]{1,0:T(8,128)(2,1)S(1)} copy-done((bf16[128,512]{1,0:T(8,128)(2,1)S(1)}, bf16[128,512]{1,0:T(8,128)(2,1)}, u32[]{:S(2)}) %copy-start.3) | copy-done | bytes 131096
  6.8 0.0 copy-start.4
  6.8 0.9 %copy-done.4 = bf16[128,512]{1,0:T(8,128)(2,1)S(1)} copy-done((bf16[128,512]{1,0:T(8,128)(2,1)S(1)}, bf16[128,512]{1,0:T(8,128)(2,1)}, u32[]{:S(2)}) %copy-start.4) | copy-done | bytes 131096
  7.7 0.0 copy-start.5
  7.7 0.9 %copy-done.5 = bf16[128,512]{1,0:T(8,128)(2,1)S(1)} copy-done((bf16[128,512]{1,0:T(8,128)(2,1)S(1)}, bf16[128,512]{1,0:T(8,128)(2,1)}, u32[]{:S(2)}) %copy-start.5) | copy-done | bytes 131096
  8.6 0.0 copy-start.6
  8.6 0.9 %copy-done.6 = bf16[128,512]{1,0:T(8,128)(2,1)S(1)} copy-done((bf16[128,512]{1,0:T(8,128)(2,1)S(1)}, bf16[128,512]{1,0:T(8,128)(2,1)}, u32[]{:S(2)}) %copy-start.6) | copy-done | bytes 131096
  9.5 0.0 copy-start.7
  9.5 0.9 %copy-done.7 = bf16[128,512]{1,0:T(8,128)(2,1)S(1)} copy-done((bf16[128,512]{1,0:T(8,128)(2,1)S(1)}, bf16[128,512]{1,0:T(8,128)(2,1)}, u32[]{:S(2)}) %copy-start.7) | copy-done | bytes 131096
  10.4 48.4 %hyena_backward.1 = (bf16[128,512]{1,0:T(8,128)(2,1)S(1)}, bf16[128,512]{1,0:T(8,128)(2,1)S(1)}, f32[128,512]{1,0:T(8,128)S(1)}) custom-call(bf16[128,512]{1,0:T(8,128)(2,1)S(1)} %copy-done.3, bf16[512,8192]{1,0:T(8,128)(2,1)S(1)} %copy-done, bf16[128,512]{1,0:T(8,128)(2,1)S(1)} %copy-done.4, bf16[128,512]{1,0:T(8,128)(2,1)S(1)} %copy-done.5, ...), custom_call_target="tpu_custom_call" | custom-call | tf_op jit(solution)/shard_map/hyena_backward/pallas_call | solution.py:339
  58.9 0.7 %copy.14 = bf16[128,512]{1,0:T(8,128)(2,1)} copy(bf16[128,512]{1,0:T(8,128)(2,1)S(1)} %get-tuple-element.6) | data formatting | bytes 262144
  59.5 0.7 %copy.15 = bf16[128,512]{1,0:T(8,128)(2,1)} copy(bf16[128,512]{1,0:T(8,128)(2,1)S(1)} %get-tuple-element.7) | data formatting | bytes 262144
  60.2 0.7 %copy.16 = f32[128,512]{1,0:T(8,128)} copy(f32[128,512]{1,0:T(8,128)S(1)} %get-tuple-element.8) | data formatting | bytes 524288
Async XLA Ops:
  0.6 3.4 %copy-start = (bf16[512,8192]{1,0:T(8,128)(2,1)S(1)}, bf16[512,8192]{1,0:T(8,128)(2,1)}, u32[]{:S(2)}) copy-start(bf16[512,8192]{1,0:T(8,128)(2,1)} %w_hbm.1) | copy-start | bytes 25165828
  4.0 0.9 %copy-start.1 = (bf16[512,256]{1,0:T(8,128)(2,1)S(1)}, bf16[512,256]{1,0:T(8,128)(2,1)}, u32[]{:S(2)}) copy-start(bf16[512,256]{1,0:T(8,128)(2,1)} %constant.5.clone.inv_hbm) | copy-start | bytes 786436
  5.0 0.9 %copy-start.2 = (bf16[256,512]{1,0:T(8,128)(2,1)S(1)}, bf16[256,512]{1,0:T(8,128)(2,1)}, u32[]{:S(2)}) copy-start(bf16[256,512]{1,0:T(8,128)(2,1)} %constant.4.clone.fwd_hbm) | copy-start | bytes 786436
  5.9 0.9 %copy-start.3 = (bf16[128,512]{1,0:T(8,128)(2,1)S(1)}, bf16[128,512]{1,0:T(8,128)(2,1)}, u32[]{:S(2)}) copy-start(bf16[128,512]{1,0:T(8,128)(2,1)} %go_hbm.1) | copy-start | bytes 393220
  6.8 0.9 %copy-start.4 = (bf16[128,512]{1,0:T(8,128)(2,1)S(1)}, bf16[128,512]{1,0:T(8,128)(2,1)}, u32[]{:S(2)}) copy-start(bf16[128,512]{1,0:T(8,128)(2,1)} %q_hbm.1) | copy-start | bytes 393220
  7.7 0.9 %copy-start.5 = (bf16[128,512]{1,0:T(8,128)(2,1)S(1)}, bf16[128,512]{1,0:T(8,128)(2,1)}, u32[]{:S(2)}) copy-start(bf16[128,512]{1,0:T(8,128)(2,1)} %key_hbm.1) | copy-start | bytes 393220
  8.6 0.9 %copy-start.6 = (bf16[128,512]{1,0:T(8,128)(2,1)S(1)}, bf16[128,512]{1,0:T(8,128)(2,1)}, u32[]{:S(2)}) copy-start(bf16[128,512]{1,0:T(8,128)(2,1)} %val_hbm.1) | copy-start | bytes 393220
  9.5 0.9 %copy-start.7 = (bf16[128,512]{1,0:T(8,128)(2,1)S(1)}, bf16[128,512]{1,0:T(8,128)(2,1)}, u32[]{:S(2)}) copy-start(bf16[128,512]{1,0:T(8,128)(2,1)} %taps_hbm.1) | copy-start | bytes 393220

commit v2 on v1

--- a/solution.py
+++ b/solution.py
@@ -13,6 +13,7 @@
 BF16 = jnp.bfloat16
 MESH = pl.DeviceIdType.MESH
 
+VMEM_GRANT = 66060288
 N_SEQ = 16
 N_CH = 16
 NZ = 8
@@ -37,12 +38,15 @@
 Z_OFF = (0, -1, -2, -3, 1, 2, 3, 4)
 PLUS = (0, 1, 2, 3, 7)
 MINUS = (0, 4, 5, 6, 7)
-HALF = LS // 2
+QUARTER = LS // 4
+A, B = (0, 2 * QUARTER), (2 * QUARTER, 2 * QUARTER)
+A0, A1, B0, B1 = ((i * QUARTER, QUARTER) for i in range(4))
+PARTS = (A, B, A0, A1, B0, B1)
 
 
 def kernel(
     go_hbm, w_hbm, q_hbm, key_hbm, val_hbm, taps_hbm, fwd_hbm, inv_hbm,
-    kg_ref, vg_ref, fg_ref,
+    out_ref,
     x_v, w_v, q_v, key_v, val_v, taps_v, fwd_v, inv_v, acc,
     ct_s, tt_s, gt_s, qt, c_r, t_r, g_r, gsp, ksp, csp, abuf, y_s, l_s, y_r, l_r,
     in_sem, w_sem, ring_send, ring_recv, a2a_send, a2a_recv,
@@ -96,27 +100,26 @@
 
     pl.semaphore_wait(barrier, 3 + N_SEQ - 1)
 
-    rows = (pl.ds(0, HALF), pl.ds(HALF, HALF))
     sent = []
 
-    def push(src, dst, half, to):
+    def push(src, dst, part, to):
         copy = pltpu.make_async_remote_copy(
-            src_ref=x_v.at[src, rows[half]],
-            dst_ref=x_v.at[dst, rows[half]],
+            src_ref=x_v.at[src, pl.ds(*part)],
+            dst_ref=x_v.at[dst, pl.ds(*part)],
             send_sem=ring_send.at[len(sent)],
-            recv_sem=ring_recv.at[dst, half],
+            recv_sem=ring_recv.at[dst, PARTS.index(part)],
             device_id={"ch": to},
             device_id_type=MESH,
         )
         copy.start()
         sent.append(copy)
 
-    def arrived(slot, half):
+    def arrived(slot, part):
         pltpu.make_async_remote_copy(
-            src_ref=x_v.at[slot, rows[half]],
-            dst_ref=x_v.at[slot, rows[half]],
+            src_ref=x_v.at[slot, pl.ds(*part)],
+            dst_ref=x_v.at[slot, pl.ds(*part)],
             send_sem=ring_send.at[0],
-            recv_sem=ring_recv.at[slot, half],
+            recv_sem=ring_recv.at[slot, PARTS.index(part)],
             device_id={"ch": up},
             device_id_type=MESH,
         ).wait_recv()
@@ -131,22 +134,29 @@
         else:
             acc[...] += part
 
-    def forward(step, base):
-        if step < 4:
-            for chain, to, last in ((PLUS, up, 0), (MINUS, down, 1)):
-                for half in (0, 1):
-                    arrived(base + chain[step], half)
-                    if step < 3 or half == last:
-                        push(base + chain[step], base + chain[step + 1], half, to)
-        else:
-            arrived(base + PLUS[4], 0)
-            arrived(base + PLUS[4], 1)
-
-    for half in (0, 1):
-        push(0, PLUS[1], half, up)
-        push(0, MINUS[1], half, down)
-    for half in (0, 1):
-        push(0, NZ, half, across)
+    def ring(step, base, whole, quarters, cross=False):
+        for chain, to, last in ((PLUS, up, quarters[0]), (MINUS, down, quarters[1])):
+            part = whole if step < 4 else last
+            arrived(base + chain[step], part)
+            if step < 3:
+                push(base + chain[step], base + chain[step + 1], part, to)
+            elif step == 3:
+                push(base + chain[step], base + chain[step + 1], last, to)
+            if cross:
+                push(base + chain[step], NZ + chain[step], part, across)
+
+    def start_ring(base, part):
+        push(base, base + PLUS[1], part, up)
+        push(base, base + MINUS[1], part, down)
+
+    ring_a = functools.partial(ring, base=0, whole=A, quarters=(A0, A1), cross=True)
+    ring_b = functools.partial(ring, base=0, whole=B, quarters=(B0, B1))
+    ring_p = functools.partial(ring, base=NZ, whole=B, quarters=(B0, B1))
+
+    start_ring(0, A)
+    push(0, NZ, B, across)
+    push(0, NZ, A, across)
+    start_ring(0, B)
 
     def scatter(block, recv, which):
         my_row = pl.ds(pl.multiple_of((s // 2) * SUB, SUB), SUB)
@@ -208,21 +218,21 @@
     ).astype(F32)
     first = lax.broadcasted_iota(jnp.int32, (1, SEG), 1) == 0
 
-    forward(1, 0)
+    ring_a(1)
+    ring_b(1)
     mult(1)
     mult(4)
-    for half in (0, 1):
-        arrived(NZ, half)
-        push(NZ, NZ + PLUS[1], half, up)
-        push(NZ, NZ + MINUS[1], half, down)
+    arrived(NZ, B)
+    start_ring(NZ, B)
+    arrived(NZ, A)
     mult(8)
-    forward(2, 0)
+    ring_a(2)
+    ring_b(2)
     mult(2)
     mult(5)
-    forward(1, NZ)
-    mult(9)
-    mult(12)
-    forward(3, 0)
+    ring_p(1)
+    ring_a(3)
+    ring_b(3)
 
     def put3(ref, cos, sin):
         ref[:, pl.ds(0, SEG)] = cos
@@ -234,8 +244,9 @@
     spec = jnp.dot(c_r[...], fwd_v[...], preferred_element_type=F32)
     put3(csp, spec[:, :SEG], spec[:, SEG:])
     mult(3)
+    ring_p(2)
     mult(6)
-    forward(2, NZ)
+    ring_a(4)
     all_in(t_r, 1)
     spec = jnp.dot(t_r[...], fwd_v[...], preferred_element_type=F32)
     before = jnp.concatenate([jnp.zeros((SUB, 2 * SEG), F32), spec[:-SUB]], 0)
@@ -244,15 +255,19 @@
         spec[:, :SEG] + sign * before[:, :SEG],
         spec[:, SEG:] + sign * before[:, SEG:],
     )
-    mult(10)
-    mult(13)
-    forward(4, 0)
+    loads[6].wait()
+    ring_b(4)
     mult(7)
-    forward(3, NZ)
-    mult(11)
-    mult(14)
-    loads[6].wait()
-    forward(4, NZ)
+    ring_p(3)
+    for slot in (9, 12, 10, 13):
+        arrived(slot, A)
+        mult(slot)
+    for slot in (11, 14):
+        arrived(slot, A)
+        mult(slot)
+    ring_p(4)
+    arrived(15, A0)
+    arrived(15, A1)
     mult(15)
 
     gt_s[...] = (acc[...] * qt[...]).astype(BF16)
@@ -317,11 +332,9 @@
     collect(l_s, l_r, 4)
 
     all_in(y_r, 3)
-    conv = y_r[...].astype(F32).T
-    kg_ref[...] = (conv * val_v[...].astype(F32)).astype(BF16)
-    vg_ref[...] = (conv * key_v[...].astype(F32)).astype(BF16)
+    out_ref[pl.ds(0, LS)] = y_r[...].astype(F32).T.astype(BF16)
     all_in(l_r, 4)
-    fg_ref[...] = l_r[...].astype(F32).T * (1.0 / math.sqrt(LS * N_SEQ))
+    out_ref[pl.ds(LS, LS)] = l_r[...].astype(F32).T.astype(BF16)
 
     for copy in sent:
         copy.wait_send()
@@ -336,15 +349,11 @@
     block = (LS, CH)
     turned = (CH, LS)
     local = (NSEG * SUB, SEG)
-    return pl.pallas_call(
+    both = pl.pallas_call(
         kernel,
-        out_shape=(
-            jax.ShapeDtypeStruct(block, BF16),
-            jax.ShapeDtypeStruct(block, BF16),
-            jax.ShapeDtypeStruct(block, F32),
-        ),
+        out_shape=jax.ShapeDtypeStruct((2 * LS, CH), BF16),
         in_specs=[any_spec] * 8,
-        out_specs=(vmem_spec,) * 3,
+        out_specs=vmem_spec,
         scratch_shapes=[
             pltpu.VMEM((N_CH, LS, CH), BF16),
             pltpu.VMEM((N_CH, CH, CH), BF16),
@@ -372,16 +381,23 @@
             pltpu.VMEM(turned, BF16),
             pltpu.SemaphoreType.DMA((7,)),
             pltpu.SemaphoreType.DMA((N_CH,)),
-            pltpu.SemaphoreType.DMA((30,)),
-            pltpu.SemaphoreType.DMA((N_CH, 2)),
+            pltpu.SemaphoreType.DMA((34,)),
+            pltpu.SemaphoreType.DMA((N_CH, 6)),
             pltpu.SemaphoreType.DMA((5,)),
             pltpu.SemaphoreType.DMA((5,)),
         ],
         compiler_params=pltpu.CompilerParams(
-            collective_id=0, has_side_effects=True, vmem_limit_bytes=40 << 20
+            collective_id=0, has_side_effects=True, vmem_limit_bytes=VMEM_GRANT
         ),
         name="hyena_backward",
     )(grad_out, out_weight, query_gate, key_branch, value_branch, filter_taps, fwd, inv)
+    conv = both[:LS].astype(F32)
+    lag = both[LS:].astype(F32)
+    return (
+        (conv * value_branch.astype(F32)).astype(BF16),
+        (conv * key_branch.astype(F32)).astype(BF16),
+        lag * (1.0 / math.sqrt(LS * N_SEQ)),
+    )
 
 
 def solution(mesh):

time: 61.2 us -> 49.5 us (0.81)
  local copies, waits for them, and re-layouts: 11.8 us -> 0.01 us
  other arithmetic: 0 us -> 1.8 us
  Pallas kernels: 48.4 us -> 46.9 us
    unnamed x19 -> x4, local copies, waits for them, and re-layouts: 11.8 us -> 0.01 us
    mul x0 -> x1, other arithmetic: none -> 1.8 us  [shards(): lag * (1.0 / math.sqrt(LS * N_SEQ))]
    pallas_call x1, Pallas kernels: 48.4 us -> 46.9 us  [shards(): pl.pallas_call(kernel, out_shape=jax.ShapeDtypeStruct((2 * LS, CH), BF16)...]
where the time goes in v2:
time: 49.5 us; the launch traced here: 49.4 us
  Pallas kernels  46.9 us (95%)
  other arithmetic  1.8 us (4%)
  between operations  0.67 us (1%)
    pallas_call x1, Pallas kernels, shards(): pl.pallas_call(kernel, out_shape=jax.ShapeDtypeStruct((2 * LS, CH), BF16)...  46.9 us
    mul x1, other arithmetic, shards(): lag * (1.0 / math.sqrt(LS * N_SEQ))  1.8 us

profile of v2, /device:TPU:1, one launch (start us, length us, event | category | flops | bytes accessed | tf_op | source)
XLA Modules:
  0.0 49.4 jit_solution(56943614117939291)
XLA Ops:
  0.6 0.0 copy-start.1
  0.6 0.0 copy-start
  0.7 46.9 %hyena_backward.1 = bf16[256,512]{1,0:T(8,128)(2,1)} custom-call(bf16[128,512]{1,0:T(8,128)(2,1)} %go_hbm.1, bf16[512,8192]{1,0:T(8,128)(2,1)} %w_hbm.1, bf16[128,512]{1,0:T(8,128)(2,1)} %q_hbm.1, bf16[128,512]{1,0:T(8,128)(2,1)} %key_hbm.1, bf16[128,512]{1,0:T(8,128)(2,1)} %val_hbm.1, bf16[128,512]{1,0:T(8,128)(2,1)} %taps_hbm.1, ...), custom_call_target="tpu_custom_call" | custom-call | tf_op jit(solution)/shard_map/hyena_backward/pallas_call | solution.py:352
  47.6 0.0 copy-done.1
  47.6 0.0 copy-done
  47.6 1.8 %convert_multiply_fusion.2 = (f32[128,512]{1,0:T(8,128)}, bf16[128,512]{1,0:T(8,128)(2,1)}, bf16[128,512]{1,0:T(8,128)(2,1)}) fusion(bf16[256,512]{1,0:T(8,128)(2,1)} %hyena_backward.1, bf16[128,512]{1,0:T(8,128)(2,1)S(1)} %copy-done, bf16[128,512]{1,0:T(8,128)(2,1)S(1)} %copy-done.1), kind=kLoop, calls=%fused_computation.4 | loop fusion | flops 589824 | bytes 1048576 | tf_op jit(solution)/shard_map/mul | solution.py:399
Async XLA Ops:
  0.6 47.0 %copy-start.1 = (bf16[128,512]{1,0:T(8,128)(2,1)S(1)}, bf16[128,512]{1,0:T(8,128)(2,1)}, u32[]{:S(2)}) copy-start(bf16[128,512]{1,0:T(8,128)(2,1)} %val_hbm.1) | copy-start | bytes 393220
  0.6 47.0 %copy-start = (bf16[128,512]{1,0:T(8,128)(2,1)S(1)}, bf16[128,512]{1,0:T(8,128)(2,1)}, u32[]{:S(2)}) copy-start(bf16[128,512]{1,0:T(8,128)(2,1)} %key_hbm.1) | copy-start | bytes 393220

commit v3 on v2

--- a/solution.py
+++ b/solution.py
@@ -38,16 +38,19 @@
 Z_OFF = (0, -1, -2, -3, 1, 2, 3, 4)
 PLUS = (0, 1, 2, 3, 7)
 MINUS = (0, 4, 5, 6, 7)
-QUARTER = LS // 4
-A, B = (0, 2 * QUARTER), (2 * QUARTER, 2 * QUARTER)
-A0, A1, B0, B1 = ((i * QUARTER, QUARTER) for i in range(4))
-PARTS = (A, B, A0, A1, B0, B1)
+CHUNK = LS // 4
+ROWS_A = (0, CHUNK)
+ROWS_B = (2 * CHUNK, 3 * CHUNK)
+RING_RECV = 50
+HOPS = tuple(
+    (dx, dy, dc) for dx in (2, 1, 3, 0) for dy in (1, 0) for dc in (0, 1) if dx or dy or dc
+)
 
 
 def kernel(
     go_hbm, w_hbm, q_hbm, key_hbm, val_hbm, taps_hbm, fwd_hbm, inv_hbm,
     out_ref,
-    x_v, w_v, q_v, key_v, val_v, taps_v, fwd_v, inv_v, acc,
+    x_v, w_v, in_v, fwd_v, inv_v, acc,
     ct_s, tt_s, gt_s, qt, c_r, t_r, g_r, gsp, ksp, csp, abuf, y_s, l_s, y_r, l_r,
     in_sem, w_sem, ring_send, ring_recv, a2a_send, a2a_recv,
 ):
@@ -66,66 +69,64 @@
     barrier = pltpu.get_barrier_semaphore()
     for peer in (up, down, across):
         pl.semaphore_signal(barrier, inc=1, device_id={"ch": peer}, device_id_type=MESH)
-    for k in range(1, N_SEQ):
+    def seq_of(hop):
+        dx, dy, dc = hop
+        return (
+            lax.rem(s // 4 + dx, 4) * 4
+            + lax.rem((s // 2) % 2 + dy, 2) * 2
+            + lax.rem(s % 2 + dc, 2)
+        )
+
+    for hop in HOPS:
         pl.semaphore_signal(
-            barrier, inc=1, device_id={"seq": lax.rem(s + k, N_SEQ)}, device_id_type=MESH
+            barrier, inc=1, device_id={"seq": seq_of(hop)}, device_id_type=MESH
         )
 
-    loads = []
-    for i, (src, dst) in enumerate((
-        (key_hbm, key_v), (val_hbm, val_v), (taps_hbm, taps_v), (q_hbm, q_v),
-        (go_hbm, x_v.at[0]), (fwd_hbm, fwd_v), (inv_hbm, inv_v),
-    )):
-        copy = pltpu.make_async_copy(src, dst, in_sem.at[i])
-        copy.start()
-        loads.append(copy)
-    w_loads = []
+    own = pltpu.make_async_copy(go_hbm, x_v.at[0], in_sem.at[0])
+    own.start()
+    for i, src in enumerate((key_hbm, val_hbm, taps_hbm, q_hbm)):
+        pltpu.make_async_copy(src, in_v.at[i], in_sem.at[1]).start()
     for slot in range(N_CH):
-        own = slot < NZ
-        chunk = ch_of(z + Z_OFF[slot % NZ], h if own else 1 - h)
-        copy = pltpu.make_async_copy(
-            w_hbm.at[:, pl.ds(pl.multiple_of(chunk * CH, CH), CH)], w_v.at[slot], w_sem.at[slot]
-        )
-        w_loads.append(copy)
-    order = (0, 1, 4, 8, 2, 5, 9, 12, 3, 6, 10, 13, 7, 11, 14, 15)
-    for slot in order:
-        w_loads[slot].start()
-
-    loads[0].wait()
-    loads[1].wait()
-    ct_s[...] = (key_v[...].astype(F32) * val_v[...].astype(F32)).T.astype(BF16)
-    loads[2].wait()
-    tt_s[...] = taps_v[...].astype(F32).T.astype(BF16)
-    loads[4].wait()
-
+        chunk = ch_of(z + Z_OFF[slot % NZ], h if slot < NZ else 1 - h)
+        pltpu.make_async_copy(
+            w_hbm.at[:, pl.ds(pl.multiple_of(chunk * CH, CH), CH)], w_v.at[slot], w_sem
+        ).start()
+    fwd_load = pltpu.make_async_copy(fwd_hbm, fwd_v, in_sem.at[2])
+    fwd_load.start()
+    inv_load = pltpu.make_async_copy(inv_hbm, inv_v, in_sem.at[3])
+    inv_load.start()
+
+    own.wait()
     pl.semaphore_wait(barrier, 3 + N_SEQ - 1)
 
-    sent = []
-
-    def push(src, dst, part, to):
-        copy = pltpu.make_async_remote_copy(
-            src_ref=x_v.at[src, pl.ds(*part)],
-            dst_ref=x_v.at[dst, pl.ds(*part)],
-            send_sem=ring_send.at[len(sent)],
-            recv_sem=ring_recv.at[dst, PARTS.index(part)],
+    keys = {}
+
+    def recv_sem(key):
+        return ring_recv.at[keys.setdefault(key, len(keys))]
+
+    def key_of(slot, row):
+        if slot % NZ == 7 and row in ROWS_B:
+            return slot
+        return slot, row
+
+    def push(src, dst, row, to, key=None):
+        pltpu.make_async_remote_copy(
+            src_ref=x_v.at[src, pl.ds(row, CHUNK)],
+            dst_ref=x_v.at[dst, pl.ds(row, CHUNK)],
+            send_sem=ring_send,
+            recv_sem=recv_sem(key or key_of(dst, row)),
             device_id={"ch": to},
             device_id_type=MESH,
-        )
-        copy.start()
-        sent.append(copy)
-
-    def arrived(slot, part):
-        pltpu.make_async_remote_copy(
-            src_ref=x_v.at[slot, pl.ds(*part)],
-            dst_ref=x_v.at[slot, pl.ds(*part)],
-            send_sem=ring_send.at[0],
-            recv_sem=ring_recv.at[slot, PARTS.index(part)],
-            device_id={"ch": up},
-            device_id_type=MESH,
-        ).wait_recv()
+        ).start()
+
+    def arrived(slot, row, rows=CHUNK, key=None):
+        part = x_v.at[slot, pl.ds(row, rows)]
+        pltpu.make_async_copy(part, part, recv_sem(key or key_of(slot, row))).wait()
+
+    def arrived_across(slot):
+        arrived(slot, 0, 2 * CHUNK, ("across", slot))
 
     def mult(slot):
-        w_loads[slot].wait()
         part = lax.dot_general(
             w_v[slot], x_v[slot], (((1,), (1,)), ((), ())), preferred_element_type=F32
         )
@@ -134,29 +135,36 @@
         else:
             acc[...] += part
 
-    def ring(step, base, whole, quarters, cross=False):
-        for chain, to, last in ((PLUS, up, quarters[0]), (MINUS, down, quarters[1])):
-            part = whole if step < 4 else last
-            arrived(base + chain[step], part)
-            if step < 3:
-                push(base + chain[step], base + chain[step + 1], part, to)
-            elif step == 3:
-                push(base + chain[step], base + chain[step + 1], last, to)
-            if cross:
-                push(base + chain[step], NZ + chain[step], part, across)
-
-    def start_ring(base, part):
-        push(base, base + PLUS[1], part, up)
-        push(base, base + MINUS[1], part, down)
-
-    ring_a = functools.partial(ring, base=0, whole=A, quarters=(A0, A1), cross=True)
-    ring_b = functools.partial(ring, base=0, whole=B, quarters=(B0, B1))
-    ring_p = functools.partial(ring, base=NZ, whole=B, quarters=(B0, B1))
-
-    start_ring(0, A)
-    push(0, NZ, B, across)
-    push(0, NZ, A, across)
-    start_ring(0, B)
+    def ring(step, base, rows, cross=False):
+        for i, row in enumerate(rows):
+            for side, (chain, to) in enumerate(((PLUS, up), (MINUS, down))):
+                if step == 4 and (i != side or not cross):
+                    continue
+                arrived(base + chain[step], row)
+                if step < 3 or (step == 3 and i == side):
+                    push(base + chain[step], base + chain[step + 1], row, to)
+                if cross:
+                    slot = NZ + chain[step]
+                    push(base + chain[step], slot, row, across, ("across", slot))
+        if step == 4 and not cross:
+            arrived(base + 7, rows[0], 2 * CHUNK)
+
+    def start_ring(base, row):
+        push(base, base + PLUS[1], row, up)
+        push(base, base + MINUS[1], row, down)
+
+    ring_a = functools.partial(ring, base=0, rows=ROWS_A, cross=True)
+    ring_b = functools.partial(ring, base=0, rows=ROWS_B)
+    ring_p = functools.partial(ring, base=NZ, rows=ROWS_B)
+
+    for row in ROWS_A:
+        start_ring(0, row)
+    for row in ROWS_B:
+        push(0, NZ, row, across)
+    for row in ROWS_A:
+        push(0, NZ, row, across, ("across", NZ))
+    for row in ROWS_B:
+        start_ring(0, row)
 
     def scatter(block, recv, which):
         my_row = pl.ds(pl.multiple_of((s // 2) * SUB, SUB), SUB)
@@ -166,8 +174,8 @@
             recv.at[my_row, my_col],
             a2a_recv.at[which],
         ).start()
-        for k in range(1, N_SEQ):
-            to = lax.rem(s + k, N_SEQ)
+        for hop in HOPS:
+            to = seq_of(hop)
             pltpu.make_async_remote_copy(
                 src_ref=block.at[pl.ds(pl.multiple_of(to * SUB, SUB), SUB)],
                 dst_ref=recv.at[my_row, my_col],
@@ -187,8 +195,8 @@
             ]
 
         pltpu.make_async_copy(piece(s), recv.at[my_row], a2a_recv.at[which]).start()
-        for k in range(1, N_SEQ):
-            to = lax.rem(s + k, N_SEQ)
+        for hop in HOPS:
+            to = seq_of(hop)
             pltpu.make_async_remote_copy(
                 src_ref=piece(to),
                 dst_ref=recv.at[my_row],
@@ -206,12 +214,12 @@
         part = block.at[pl.ds(0, rows_sent)]
         pltpu.make_async_copy(part, part, a2a_send.at[which]).wait()
 
+    pltpu.make_async_copy(in_v, in_v, in_sem.at[1]).wait()
+    ct_s[...] = (in_v[0].astype(F32) * in_v[1].astype(F32)).T.astype(BF16)
     scatter(ct_s, c_r, 0)
+    tt_s[...] = in_v[2].astype(F32).T.astype(BF16)
     scatter(tt_s, t_r, 1)
-
-    loads[3].wait()
-    qt[...] = q_v[...].astype(F32).T
-    mult(0)
+    qt[...] = in_v[3].astype(F32).T
 
     sign = jnp.where(
         lax.broadcasted_iota(jnp.int32, (1, SEG), 1) % 2 == 0, 1.0, -1.0
@@ -220,33 +228,38 @@
 
     ring_a(1)
     ring_b(1)
+    for row in ROWS_B:
+        arrived(NZ, row)
+        start_ring(NZ, row)
+    pltpu.make_async_copy(w_v, w_v, w_sem).wait()
+    mult(0)
     mult(1)
     mult(4)
-    arrived(NZ, B)
-    start_ring(NZ, B)
-    arrived(NZ, A)
-    mult(8)
     ring_a(2)
     ring_b(2)
+    ring_p(1)
     mult(2)
     mult(5)
-    ring_p(1)
+    arrived_across(NZ)
+    mult(8)
     ring_a(3)
     ring_b(3)
+    ring_p(2)
 
     def put3(ref, cos, sin):
         ref[:, pl.ds(0, SEG)] = cos
         ref[:, pl.ds(SEG, SEG)] = jnp.where(first, 0.0, sin)
         ref[:, pl.ds(2 * SEG, SEG)] = jnp.where(first, sin, cos)
 
-    loads[5].wait()
+    fwd_load.wait()
     all_in(c_r, 0)
     spec = jnp.dot(c_r[...], fwd_v[...], preferred_element_type=F32)
     put3(csp, spec[:, :SEG], spec[:, SEG:])
     mult(3)
-    ring_p(2)
     mult(6)
     ring_a(4)
+    ring_b(4)
+    ring_p(3)
     all_in(t_r, 1)
     spec = jnp.dot(t_r[...], fwd_v[...], preferred_element_type=F32)
     before = jnp.concatenate([jnp.zeros((SUB, 2 * SEG), F32), spec[:-SUB]], 0)
@@ -255,20 +268,15 @@
         spec[:, :SEG] + sign * before[:, :SEG],
         spec[:, SEG:] + sign * before[:, SEG:],
     )
-    loads[6].wait()
-    ring_b(4)
+    inv_load.wait()
     mult(7)
-    ring_p(3)
     for slot in (9, 12, 10, 13):
-        arrived(slot, A)
-        mult(slot)
-    for slot in (11, 14):
-        arrived(slot, A)
+        arrived_across(slot)
         mult(slot)
     ring_p(4)
-    arrived(15, A0)
-    arrived(15, A1)
-    mult(15)
+    for slot in (11, 14, 15):
+        arrived_across(slot)
+        mult(slot)
 
     gt_s[...] = (acc[...] * qt[...]).astype(BF16)
     scatter(gt_s, g_r, 2)
@@ -336,8 +344,9 @@
     all_in(l_r, 4)
     out_ref[pl.ds(LS, LS)] = l_r[...].astype(F32).T.astype(BF16)
 
-    for copy in sent:
-        copy.wait_send()
+    all_sent = x_v.at[pl.ds(0, N_CH - 1)]
+    pltpu.make_async_copy(all_sent, all_sent, ring_send).wait()
+    assert len(keys) == RING_RECV
     for which, block in enumerate((ct_s, tt_s, gt_s, y_s, l_s)):
         all_out(block, which)
 
@@ -351,16 +360,13 @@
     local = (NSEG * SUB, SEG)
     both = pl.pallas_call(
         kernel,
-        out_shape=jax.ShapeDtypeStruct((2 * LS, CH), BF16),
+        out_shape=pltpu.VMEM((2 * LS, CH), BF16),
         in_specs=[any_spec] * 8,
         out_specs=vmem_spec,
         scratch_shapes=[
             pltpu.VMEM((N_CH, LS, CH), BF16),
             pltpu.VMEM((N_CH, CH, CH), BF16),
-            pltpu.VMEM(block, BF16),
-            pltpu.VMEM(block, BF16),
-            pltpu.VMEM(block, BF16),
-            pltpu.VMEM(block, BF16),
+            pltpu.VMEM((4, *block), BF16),
             pltpu.VMEM((SEG, 2 * SEG), BF16),
             pltpu.VMEM((2 * SEG, SEG), BF16),
             pltpu.VMEM(turned, F32),
@@ -379,10 +385,10 @@
             pltpu.VMEM(local, BF16),
             pltpu.VMEM(turned, BF16),
             pltpu.VMEM(turned, BF16),
-            pltpu.SemaphoreType.DMA((7,)),
-            pltpu.SemaphoreType.DMA((N_CH,)),
-            pltpu.SemaphoreType.DMA((34,)),
-            pltpu.SemaphoreType.DMA((N_CH, 6)),
+            pltpu.SemaphoreType.DMA((4,)),
+            pltpu.SemaphoreType.DMA,
+            pltpu.SemaphoreType.DMA,
+            pltpu.SemaphoreType.DMA((RING_RECV,)),
             pltpu.SemaphoreType.DMA((5,)),
             pltpu.SemaphoreType.DMA((5,)),
         ],

time: 49.5 us -> 44 us (0.89)
  Pallas kernels: 46.9 us -> 42.4 us
  other arithmetic: 1.8 us -> 0.83 us
    pallas_call x1, Pallas kernels: 46.9 us -> 42.4 us  [shards(): pl.pallas_call(kernel, out_shape=pltpu.VMEM((2 * LS, CH), BF16), in_specs...]
    mul x1, other arithmetic: 1.8 us -> 0.83 us  [shards(): lag * (1.0 / math.sqrt(LS * N_SEQ))]
where the time goes in v3:
time: 44 us; the launch traced here: 43.9 us
  Pallas kernels  42.4 us (96%)
  other arithmetic  0.83 us (2%)
  between operations  0.67 us (2%)
    pallas_call x1, Pallas kernels, shards(): pl.pallas_call(kernel, out_shape=pltpu.VMEM((2 * LS, CH), BF16), in_specs...  42.4 us

profile of v3, /device:TPU:1, one launch (start us, length us, event | category | flops | bytes accessed | tf_op | source)
XLA Modules:
  0.0 43.9 jit_solution(3023276559199458024)
XLA Ops:
  0.6 0.0 copy-start.1
  0.6 0.0 copy-start
  0.7 42.4 %hyena_backward.1 = bf16[256,512]{1,0:T(8,128)(2,1)S(1)} custom-call(bf16[128,512]{1,0:T(8,128)(2,1)} %go_hbm.1, bf16[512,8192]{1,0:T(8,128)(2,1)} %w_hbm.1, bf16[128,512]{1,0:T(8,128)(2,1)} %q_hbm.1, bf16[128,512]{1,0:T(8,128)(2,1)} %key_hbm.1, bf16[128,512]{1,0:T(8,128)(2,1)} %val_hbm.1, bf16[128,512]{1,0:T(8,128)(2,1)} %taps_hbm.1, ...), custom_call_target="tpu_custom_call" | custom-call | tf_op jit(solution)/shard_map/hyena_backward/pallas_call | solution.py:361
  43.1 0.0 copy-done.1
  43.1 0.0 copy-done
  43.1 0.8 %convert_multiply_fusion.2 = (f32[128,512]{1,0:T(8,128)}, bf16[128,512]{1,0:T(8,128)(2,1)}, bf16[128,512]{1,0:T(8,128)(2,1)}) fusion(bf16[256,512]{1,0:T(8,128)(2,1)S(1)} %hyena_backward.1, bf16[128,512]{1,0:T(8,128)(2,1)S(1)} %copy-done, bf16[128,512]{1,0:T(8,128)(2,1)S(1)} %copy-done.1), kind=kLoop, calls=%fused_computation.4 | loop fusion | flops 589824 | bytes 1048576 | tf_op jit(solution)/shard_map/mul | solution.py:405
Async XLA Ops:
  0.6 42.5 %copy-start.1 = (bf16[128,512]{1,0:T(8,128)(2,1)S(1)}, bf16[128,512]{1,0:T(8,128)(2,1)}, u32[]{:S(2)}) copy-start(bf16[128,512]{1,0:T(8,128)(2,1)} %val_hbm.1) | copy-start | bytes 393220
  0.6 42.5 %copy-start = (bf16[128,512]{1,0:T(8,128)(2,1)S(1)}, bf16[128,512]{1,0:T(8,128)(2,1)}, u32[]{:S(2)}) copy-start(bf16[128,512]{1,0:T(8,128)(2,1)} %key_hbm.1) | copy-start | bytes 393220

commit v4 on v3

v4 whole, which is shorter than its diff:
```python
import functools
import math

import jax
import jax.numpy as jnp
import numpy as np
from jax import lax
from jax.experimental import pallas as pl
from jax.experimental.pallas import tpu as pltpu
from jax.sharding import PartitionSpec as P

F32 = jnp.float32
BF16 = jnp.bfloat16
MESH = pl.DeviceIdType.MESH

VMEM_GRANT = 66060288
N_SEQ = 16
N_CH = 16
NZ = 8
LS = 128
CH = 512
SUB = CH // N_SEQ
SEG = 256
NSEG = LS * N_SEQ // SEG


def tables():
    m = 2 * SEG
    t = np.arange(SEG)
    theta = 2.0 * np.pi * ((t[:, None] * t[None, :]) % m) / m
    fwd = np.concatenate([np.cos(theta), np.sin(theta)], 1)
    fwd[:, SEG] = np.where(t % 2 == 0, 1.0, -1.0)
    weight = np.full((m, 1), 2.0 / m)
    weight[0] = weight[SEG] = 1.0 / m
    return jnp.asarray(fwd, BF16), jnp.asarray(weight * fwd.T, BF16)


Z_OFF = (0, -1, -2, -3, 1, 2, 3, -4)
FIRST, SECOND, LAST = 0, 3, 7
CHUNK = LS // 4
ROWS_A = (0, CHUNK)
ROWS_B = (2 * CHUNK, 3 * CHUNK)
EARLY = 1
HOPS = tuple(
    (dx, dy, dc) for dx in (2, 1, 3, 0) for dy in (1, 0) for dc in (0, 1) if dx or dy or dc
)


def kernel(
    go_hbm, w_hbm, q_hbm, key_hbm, val_hbm, taps_hbm, fwd_hbm, inv_hbm,
    out_ref,
    x_v, w_v, in_v, fwd_v, inv_v, acc,
    ct_s, tt_s, gt_s, qt, c_r, t_r, g_r, gsp, ksp, csp, abuf, y_s, l_s, y_r, l_r,
    in_sem, w_sem, ring_send, own_recv, pair_recv, across_recv, a2a_send, a2a_recv,
):
    s = lax.axis_index("seq")
    c = lax.axis_index("ch")
    z, h = lax.div(c, 2), lax.rem(c, 2)

    def ch_of(zz, hh):
        return lax.rem(zz + 2 * NZ, NZ) * 2 + hh

    def upward(zz):
        return lax.rem(lax.div(zz + 2, 4), 2)

    mine = upward(z)
    step_z = 2 * mine - 1
    ahead, behind = ch_of(z + step_z, h), ch_of(z - step_z, h)
    same_ahead = 1 - (mine + upward(lax.div(ahead, 2))) % 2
    same_behind = 1 - (mine + upward(lax.div(behind, 2))) % 2
    across = z * 2 + (1 - h)

    barrier = pltpu.get_barrier_semaphore()
    for peer in (ahead, behind, across):
        pl.semaphore_signal(barrier, inc=1, device_id={"ch": peer}, device_id_type=MESH)
    pair_in_seq, core = lax.div(s, 2), lax.rem(s, 2)
    x, y_lo = lax.div(pair_in_seq, 2), lax.rem(pair_in_seq, 2)

    def pair_of(hop):
        dx, dy, dc = hop
        return lax.rem(x + dx, 4) * 2 + lax.rem(y_lo + dy, 2), lax.rem(core + dc, 2)

    def seq_of(hop):
        pair, of_pair = pair_of(hop)
        return pair * 2 + of_pair

    for hop in HOPS:
        pl.semaphore_signal(
            barrier, inc=1, device_id={"seq": seq_of(hop)}, device_id_type=MESH
        )

    own = pltpu.make_async_copy(go_hbm, x_v.at[0], in_sem.at[0])
    own.start()
    for i, src in enumerate((key_hbm, val_hbm, taps_hbm, q_hbm)):
        pltpu.make_async_copy(src, in_v.at[i], in_sem.at[1]).start()
    for slot in range(N_CH):
        chunk = ch_of(z + step_z * Z_OFF[slot % NZ], h if slot < NZ else 1 - h)
        pltpu.make_async_copy(
            w_hbm.at[:, pl.ds(pl.multiple_of(chunk * CH, CH), CH)], w_v.at[slot], w_sem
        ).start()
    fwd_load = pltpu.make_async_copy(fwd_hbm, fwd_v, in_sem.at[2])
    fwd_load.start()
    inv_load = pltpu.make_async_copy(inv_hbm, inv_v, in_sem.at[3])
    inv_load.start()

    own.wait()
    pl.semaphore_wait(barrier, 3 + N_SEQ - 1)

    def recv_sem(base, slot, row):
        if base == 0:
            return own_recv.at[slot, row // CHUNK]
        return pair_recv.at[slot, row // CHUNK - 2]

    def push(base, src, dst, row, to, send):
        pltpu.make_async_remote_copy(
            src_ref=x_v.at[base + src, pl.ds(row, CHUNK)],
            dst_ref=x_v.at[base + dst, pl.ds(row, CHUNK)],
            send_sem=ring_send.at[send],
            recv_sem=recv_sem(base, dst, row),
            device_id={"ch": to},
            device_id_type=MESH,
        ).start()

    def push_across(slot, row):
        pltpu.make_async_remote_copy(
            src_ref=x_v.at[slot, pl.ds(row, CHUNK)],
            dst_ref=x_v.at[NZ + slot, pl.ds(row, CHUNK)],
            send_sem=ring_send.at[1],
            recv_sem=across_recv.at[slot] if row in ROWS_A else recv_sem(NZ, 0, row),
            device_id={"ch": across},
            device_id_type=MESH,
        ).start()

    def arrived(base, slot, row):
        part = x_v.at[base + slot, pl.ds(row, CHUNK)]
        pltpu.make_async_copy(part, part, recv_sem(base, slot, row)).wait()

    def arrived_across(slot):
        part = x_v.at[NZ + slot, pl.ds(0, 2 * CHUNK)]
        pltpu.make_async_copy(part, part, across_recv.at[slot]).wait()

    def mult(slot):
        acc[...] += lax.dot_general(
            w_v[slot], x_v[slot], (((1,), (1,)), ((), ())), preferred_element_type=F32
        )

    def mult_pair(slot, wait=False):
        @pl.loop(0, 2)
        def _(side):
            if wait:
                arrived_across(slot - NZ + 3 * side)
            mult(slot + 3 * side)

    slot_ahead = FIRST + 3 * (1 - same_ahead)
    slot_behind = FIRST + 3 * same_behind
    goes_on = (same_ahead == 1, same_behind == 0)

    def start_ring(base, row):
        push(base, 0, slot_ahead + 1, row, ahead, 0)
        push(base, 0, slot_behind + 1, row, behind, 0)

    def ring(side, step, base, rows):
        slot = LAST if step == 4 else side + step
        to, there = (ahead, slot_ahead) if side == FIRST else (behind, slot_behind)
        for row in rows:
            arrived(base, slot, row)
            if step < 3:
                push(base, slot, there + step + 1, row, to, 0)
            elif step == 3:

                @pl.when(goes_on[side // 3])
                def _():
                    push(base, slot, LAST, row, to, 2 + side // 3)

            if base == 0 and row in ROWS_A:
                push_across(slot, row)

    def both_sides(step, base, rows):
        for row in rows:
            for side in (FIRST, SECOND)[: 1 if step == 4 else 2]:
                ring(side, step, base, (row,))

    def ring_own(step):
        both_sides(step, 0, ROWS_A)
        both_sides(step, 0, ROWS_B)

    def ring_pair(step):
        both_sides(step, NZ, ROWS_B)

    for row in ROWS_A:
        start_ring(0, row)
    for row in ROWS_B:
        push_across(0, row)
    for row in ROWS_A:
        push_across(0, row)
    for row in ROWS_B:
        start_ring(0, row)

    def scatter(block, recv, which):
        my_row = pl.ds(pl.multiple_of(pair_in_seq * SUB, SUB), SUB)
        my_col = pl.ds(pl.multiple_of(core * LS, LS), LS)
        pltpu.make_async_copy(
            block.at[pl.ds(pl.multiple_of(s * SUB, SUB), SUB)],
            recv.at[my_row, my_col],
            a2a_recv.at[which],
        ).start()
        for hop in HOPS:
            to = seq_of(hop)
            pltpu.make_async_remote_copy(
                src_ref=block.at[pl.ds(pl.multiple_of(to * SUB, SUB), SUB)],
                dst_ref=recv.at[my_row, my_col],
                send_sem=a2a_send.at[which],
                recv_sem=a2a_recv.at[which],
                device_id={"seq": to},
                device_id_type=MESH,
            ).start()

    def collect(block, recv, which):
        my_row = pl.ds(pl.multiple_of(s * SUB, SUB), SUB)

        def piece(pair, of_pair):
            return block.at[
                pl.ds(pl.multiple_of(pair * SUB, SUB), SUB),
                pl.ds(pl.multiple_of(of_pair * LS, LS), LS),
            ]

        pltpu.make_async_copy(piece(pair_in_seq, core), recv.at[my_row], a2a_recv.at[which]).start()
        def give(pair, of_pair):
            pltpu.make_async_remote_copy(
                src_ref=piece(pair, of_pair),
                dst_ref=recv.at[my_row],
                send_sem=a2a_send.at[which],
                recv_sem=a2a_recv.at[which],
                device_id={"seq": pair * 2 + of_pair},
                device_id_type=MESH,
            ).start()

        pl.when(s != EARLY)(lambda: give(EARLY // 2, EARLY % 2))
        for hop in HOPS:
            pl.when(seq_of(hop) != EARLY)(functools.partial(give, *pair_of(hop)))

    def all_in(recv, which):
        pltpu.make_async_copy(recv, recv, a2a_recv.at[which]).wait()

    def all_out(block, which):
        rows_sent = block.shape[0] - block.shape[0] // N_SEQ
        part = block.at[pl.ds(0, rows_sent)]
        pltpu.make_async_copy(part, part, a2a_send.at[which]).wait()

    pltpu.make_async_copy(in_v, in_v, in_sem.at[1]).wait()
    ct_s[...] = (in_v[0].astype(F32) * in_v[1].astype(F32)).T.astype(BF16)
    scatter(ct_s, c_r, 0)
    tt_s[...] = in_v[2].astype(F32).T.astype(BF16)
    scatter(tt_s, t_r, 1)
    qt[...] = in_v[3].astype(F32).T

    sign = jnp.where(
        lax.broadcasted_iota(jnp.int32, (1, SEG), 1) % 2 == 0, 1.0, -1.0
    ).astype(F32)
    first = lax.broadcasted_iota(jnp.int32, (1, SEG), 1) == 0

    ring_own(1)
    for row in ROWS_B:
        arrived(NZ, 0, row)
        start_ring(NZ, row)
    pltpu.make_async_copy(w_v, w_v, w_sem).wait()
    acc[...] = jnp.zeros_like(acc)
    mult(0)
    mult_pair(1)
    ring_own(2)
    ring_pair(1)
    mult_pair(2)
    arrived_across(0)
    mult(8)
    ring_own(3)
    ring_pair(2)

    def put3(ref, cos, sin):
        ref[:, pl.ds(0, SEG)] = cos
        ref[:, pl.ds(SEG, SEG)] = jnp.where(first, 0.0, sin)
        ref[:, pl.ds(2 * SEG, SEG)] = jnp.where(first, sin, cos)

    fwd_load.wait()
    all_in(c_r, 0)
    spec = jnp.dot(c_r[...], fwd_v[...], preferred_element_type=F32)
    put3(csp, spec[:, :SEG], spec[:, SEG:])
    mult_pair(3)
    ring_own(4)
    ring_pair(3)
    all_in(t_r, 1)
    spec = jnp.dot(t_r[...], fwd_v[...], preferred_element_type=F32)
    before = jnp.concatenate([jnp.zeros((SUB, 2 * SEG), F32), spec[:-SUB]], 0)
    put3(
        ksp,
        spec[:, :SEG] + sign * before[:, :SEG],
        spec[:, SEG:] + sign * before[:, SEG:],
    )
    inv_load.wait()
    mult(7)
    mult_pair(NZ + 1, True)
    mult_pair(NZ + 2, True)
    ring_pair(4)
    mult_pair(NZ + 3, True)
    arrived_across(LAST)
    mult(NZ + LAST)

    gt_s[...] = (acc[...] * qt[...]).astype(BF16)
    scatter(gt_s, g_r, 2)
    all_in(g_r, 2)
    gsp[...] = jnp.dot(g_r[...], fwd_v[...], preferred_element_type=F32)

    tile = 8
    spots = [(row, col) for row in range(0, SUB, tile) for col in range(0, SEG, 128)]

    def at(ref, seg, row, col):
        return ref[pl.ds(seg * SUB + row, tile), pl.ds(col, 128)]

    def put(seg, row, col, value):
        abuf[pl.ds(seg * SUB + row, tile), pl.ds(col, 128)] = value.astype(BF16)

    def correlate(ref, row, col):
        g = [(at(gsp, i, row, col), at(gsp, i, row, SEG + col)) for i in range(NSEG)]
        out = [None] * NSEG
        for j in range(NSEG):
            ka, kb, k2 = (at(ref, j, row, part * SEG + col) for part in range(3))
            for i in range(NSEG - j):
                ga, gb = g[i + j]
                re, im = ga * ka + gb * kb, gb * k2 - ga * kb
                out[i] = (re, im) if out[i] is None else (out[i][0] + re, out[i][1] + im)
        return out

    for row, col in spots:
        for j, (re, im) in enumerate(correlate(ksp, row, col)):
            put(j, row, col, re)
            put(j, row, SEG + col, im)

    y_s[...] = jnp.dot(abuf[...], inv_v[...], preferred_element_type=F32).astype(BF16)
    collect(y_s, y_r, 3)

    lane_sign = sign[:, :128]

    for row, col in spots:
        lags = correlate(csp, row, col)
        for r, (re, im) in enumerate(lags):
            if r + 1 < NSEG:
                re += lane_sign * lags[r + 1][0]
                im += lane_sign * lags[r + 1][1]
            put(r, row, col, re)
            put(r, row, SEG + col, im)

    l_s[...] = jnp.dot(abuf[...], inv_v[...], preferred_element_type=F32).astype(BF16)
    collect(l_s, l_r, 4)

    all_in(y_r, 3)
    out_ref[pl.ds(0, LS)] = y_r[...].astype(F32).T.astype(BF16)
    all_in(l_r, 4)
    out_ref[pl.ds(LS, LS)] = l_r[...].astype(F32).T.astype(BF16)

    def drain(part, i):
        pltpu.make_async_copy(part, part, ring_send.at[i]).wait()

    drain(x_v.at[pl.ds(0, 9)], 0)
    drain(x_v.at[pl.ds(0, 9), pl.ds(0, 2 * CHUNK)], 1)
    for side in (0, 1):

        @pl.when(goes_on[side])
        def _():
            drain(x_v.at[pl.ds(0, 3), pl.ds(0, 2 * CHUNK)], 2 + side)

    for which, block in enumerate((ct_s, tt_s, gt_s, y_s, l_s)):
        all_out(block, which)


def shards(grad_out, out_weight, query_gate, key_branch, value_branch, filter_taps):
    fwd, inv = tables()
    any_spec = pl.BlockSpec(memory_space=pl.ANY)
    vmem_spec = pl.BlockSpec(memory_space=pltpu.VMEM)
    block = (LS, CH)
    turned = (CH, LS)
    local = (NSEG * SUB, SEG)
    both = pl.pallas_call(
        kernel,
        out_shape=pltpu.VMEM((2 * LS, CH), BF16),
        in_specs=[any_spec] * 8,
        out_specs=vmem_spec,
        scratch_shapes=[
            pltpu.VMEM((N_CH, LS, CH), BF16),
            pltpu.VMEM((N_CH, CH, CH), BF16),
            pltpu.VMEM((4, *block), BF16),
            pltpu.VMEM((SEG, 2 * SEG), BF16),
            pltpu.VMEM((2 * SEG, SEG), BF16),
            pltpu.VMEM(turned, F32),
            pltpu.VMEM(turned, BF16),
            pltpu.VMEM(turned, BF16),
            pltpu.VMEM(turned, BF16),
            pltpu.VMEM(turned, F32),
            pltpu.VMEM(local, BF16),
            pltpu.VMEM(local, BF16),
            pltpu.VMEM(local, BF16),
            pltpu.VMEM((NSEG * SUB, 2 * SEG), F32),
            pltpu.VMEM((NSEG * SUB, 3 * SEG), F32),
            pltpu.VMEM((NSEG * SUB, 3 * SEG), F32),
            pltpu.VMEM((NSEG * SUB, 2 * SEG), BF16),
            pltpu.VMEM(local, BF16),
            pltpu.VMEM(local, BF16),
            pltpu.VMEM(turned, BF16),
            pltpu.VMEM(turned, BF16),
            pltpu.SemaphoreType.DMA((4,)),
            pltpu.SemaphoreType.DMA,
            pltpu.SemaphoreType.DMA((4,)),
            pltpu.SemaphoreType.DMA((NZ, 4)),
            pltpu.SemaphoreType.DMA((NZ, 2)),
            pltpu.SemaphoreType.DMA((NZ,)),
            pltpu.SemaphoreType.DMA((5,)),
            pltpu.SemaphoreType.DMA((5,)),
        ],
        compiler_params=pltpu.CompilerParams(
            collective_id=0, has_side_effects=True, vmem_limit_bytes=VMEM_GRANT
        ),
        name="hyena_backward",
    )(grad_out, out_weight, query_gate, key_branch, value_branch, filter_taps, fwd, inv)
    conv = both[:LS].astype(F32)
    lag = both[LS:].astype(F32)
    return (
        (conv * value_branch.astype(F32)).astype(BF16),
        (conv * key_branch.astype(F32)).astype(BF16),
        lag * (1.0 / math.sqrt(LS * N_SEQ)),
    )


def solution(mesh):
    spec = P("seq", "ch")
    return jax.shard_map(
        shards,
        mesh=mesh,
        in_specs=(spec, P("ch", None), spec, spec, spec, spec),
        out_specs=(spec, spec, spec),
        check_vma=False,
    )
```

time: 44 us -> 43.3 us (0.984)
  Pallas kernels: 42.4 us -> 41.7 us
    pallas_call x1, Pallas kernels: 42.4 us -> 41.7 us  [shards(): pl.pallas_call(kernel, out_shape=pltpu.VMEM((2 * LS, CH), BF16), in_specs...]
where the time goes in v4:
time: 43.3 us; the launch traced here: 43.2 us
  Pallas kernels  41.7 us (96%)
  other arithmetic  0.83 us (2%)
  between operations  0.67 us (2%)
    pallas_call x1, Pallas kernels, shards(): pl.pallas_call(kernel, out_shape=pltpu.VMEM((2 * LS, CH), BF16), in_specs...  41.7 us

profile of v4, /device:TPU:1, one launch (start us, length us, event | category | flops | bytes accessed | tf_op | source)
XLA Modules:
  0.0 43.2 jit_solution(10522071420183089448)
XLA Ops:
  0.6 0.0 copy-start.1
  0.6 0.0 copy-start
  0.7 41.7 %hyena_backward.1 = bf16[256,512]{1,0:T(8,128)(2,1)S(1)} custom-call(bf16[128,512]{1,0:T(8,128)(2,1)} %go_hbm.1, bf16[512,8192]{1,0:T(8,128)(2,1)} %w_hbm.1, bf16[128,512]{1,0:T(8,128)(2,1)} %q_hbm.1, bf16[128,512]{1,0:T(8,128)(2,1)} %key_hbm.1, bf16[128,512]{1,0:T(8,128)(2,1)} %val_hbm.1, bf16[128,512]{1,0:T(8,128)(2,1)} %taps_hbm.1, ...), custom_call_target="tpu_custom_call" | custom-call | tf_op jit(solution)/shard_map/hyena_backward/pallas_call | solution.py:381
  42.3 0.0 copy-done.1
  42.3 0.0 copy-done
  42.3 0.8 %convert_multiply_fusion.2 = (f32[128,512]{1,0:T(8,128)}, bf16[128,512]{1,0:T(8,128)(2,1)}, bf16[128,512]{1,0:T(8,128)(2,1)}) fusion(bf16[256,512]{1,0:T(8,128)(2,1)S(1)} %hyena_backward.1, bf16[128,512]{1,0:T(8,128)(2,1)S(1)} %copy-done, bf16[128,512]{1,0:T(8,128)(2,1)S(1)} %copy-done.1), kind=kLoop, calls=%fused_computation.4 | loop fusion | flops 589824 | bytes 1048576 | tf_op jit(solution)/shard_map/mul | solution.py:427
Async XLA Ops:
  0.6 41.7 %copy-start.1 = (bf16[128,512]{1,0:T(8,128)(2,1)S(1)}, bf16[128,512]{1,0:T(8,128)(2,1)}, u32[]{:S(2)}) copy-start(bf16[128,512]{1,0:T(8,128)(2,1)} %val_hbm.1) | copy-start | bytes 393220
  0.6 41.7 %copy-start = (bf16[128,512]{1,0:T(8,128)(2,1)S(1)}, bf16[128,512]{1,0:T(8,128)(2,1)}, u32[]{:S(2)}) copy-start(bf16[128,512]{1,0:T(8,128)(2,1)} %key_hbm.1) | copy-start | bytes 393220

commit v5 on v4

--- a/solution.py
+++ b/solution.py
@@ -37,10 +37,11 @@
 
 Z_OFF = (0, -1, -2, -3, 1, 2, 3, -4)
 FIRST, SECOND, LAST = 0, 3, 7
-CHUNK = LS // 4
-ROWS_A = (0, CHUNK)
-ROWS_B = (2 * CHUNK, 3 * CHUNK)
-EARLY = 1
+CHUNKS = 4
+CHUNK = LS // CHUNKS
+N_A = 2
+ROWS = tuple(range(0, LS, CHUNK))
+ROWS_A, ROWS_B = ROWS[:N_A], ROWS[N_A:]
 HOPS = tuple(
     (dx, dy, dc) for dx in (2, 1, 3, 0) for dy in (1, 0) for dc in (0, 1) if dx or dy or dc
 )
@@ -109,7 +110,7 @@
     def recv_sem(base, slot, row):
         if base == 0:
             return own_recv.at[slot, row // CHUNK]
-        return pair_recv.at[slot, row // CHUNK - 2]
+        return pair_recv.at[slot, row // CHUNK - N_A]
 
     def push(base, src, dst, row, to, send):
         pltpu.make_async_remote_copy(
@@ -136,7 +137,7 @@
         pltpu.make_async_copy(part, part, recv_sem(base, slot, row)).wait()
 
     def arrived_across(slot):
-        part = x_v.at[NZ + slot, pl.ds(0, 2 * CHUNK)]
+        part = x_v.at[NZ + slot, pl.ds(0, N_A * CHUNK)]
         pltpu.make_async_copy(part, part, across_recv.at[slot]).wait()
 
     def mult(slot):
@@ -215,29 +216,35 @@
                 device_id_type=MESH,
             ).start()
 
+    def piece(block, pair, of_pair):
+        return block.at[
+            pl.ds(pl.multiple_of(pair * SUB, SUB), SUB),
+            pl.ds(pl.multiple_of(of_pair * LS, LS), LS),
+        ]
+
+    def give(block, recv, which, pair, of_pair):
+        pltpu.make_async_remote_copy(
+            src_ref=piece(block, pair, of_pair),
+            dst_ref=recv.at[pl.ds(pl.multiple_of(s * SUB, SUB), SUB)],
+            send_sem=a2a_send.at[which],
+            recv_sem=a2a_recv.at[which],
+            device_id={"seq": pair * 2 + of_pair},
+            device_id_type=MESH,
+        ).start()
+
+    def collect_first(block, recv, which):
+        for of_pair in (1, 0):
+            pl.when(s != of_pair)(functools.partial(give, block, recv, which, 0, of_pair))
+
     def collect(block, recv, which):
-        my_row = pl.ds(pl.multiple_of(s * SUB, SUB), SUB)
-
-        def piece(pair, of_pair):
-            return block.at[
-                pl.ds(pl.multiple_of(pair * SUB, SUB), SUB),
-                pl.ds(pl.multiple_of(of_pair * LS, LS), LS),
-            ]
-
-        pltpu.make_async_copy(piece(pair_in_seq, core), recv.at[my_row], a2a_recv.at[which]).start()
-        def give(pair, of_pair):
-            pltpu.make_async_remote_copy(
-                src_ref=piece(pair, of_pair),
-                dst_ref=recv.at[my_row],
-                send_sem=a2a_send.at[which],
-                recv_sem=a2a_recv.at[which],
-                device_id={"seq": pair * 2 + of_pair},
-                device_id_type=MESH,
-            ).start()
-
-        pl.when(s != EARLY)(lambda: give(EARLY // 2, EARLY % 2))
         for hop in HOPS:
-            pl.when(seq_of(hop) != EARLY)(functools.partial(give, *pair_of(hop)))
+            pair, of_pair = pair_of(hop)
+            pl.when(pair != 0)(functools.partial(give, block, recv, which, pair, of_pair))
+        pltpu.make_async_copy(
+            piece(block, pair_in_seq, core),
+            recv.at[pl.ds(pl.multiple_of(s * SUB, SUB), SUB)],
+            a2a_recv.at[which],
+        ).start()
 
     def all_in(recv, which):
         pltpu.make_async_copy(recv, recv, a2a_recv.at[which]).wait()
@@ -318,37 +325,52 @@
     def put(seg, row, col, value):
         abuf[pl.ds(seg * SUB + row, tile), pl.ds(col, 128)] = value.astype(BF16)
 
-    def correlate(ref, row, col):
+    def correlate(ref, row, col, wanted):
         g = [(at(gsp, i, row, col), at(gsp, i, row, SEG + col)) for i in range(NSEG)]
-        out = [None] * NSEG
+        out = dict.fromkeys(wanted)
         for j in range(NSEG):
             ka, kb, k2 = (at(ref, j, row, part * SEG + col) for part in range(3))
-            for i in range(NSEG - j):
-                ga, gb = g[i + j]
-                re, im = ga * ka + gb * kb, gb * k2 - ga * kb
-                out[i] = (re, im) if out[i] is None else (out[i][0] + re, out[i][1] + im)
+            for i in wanted:
+                if i + j < NSEG:
+                    ga, gb = g[i + j]
+                    re, im = ga * ka + gb * kb, gb * k2 - ga * kb
+                    out[i] = (re, im) if out[i] is None else (out[i][0] + re, out[i][1] + im)
         return out
 
-    for row, col in spots:
-        for j, (re, im) in enumerate(correlate(ksp, row, col)):
-            put(j, row, col, re)
-            put(j, row, SEG + col, im)
-
-    y_s[...] = jnp.dot(abuf[...], inv_v[...], preferred_element_type=F32).astype(BF16)
+    def grads(segs, base):
+        for row, col in spots:
+            for j, (re, im) in correlate(ksp, row, col, segs).items():
+                put(base + j, row, col, re)
+                put(base + j, row, SEG + col, im)
+
+    lane_sign = sign[:, :128]
+
+    def lags(segs, base):
+        for row, col in spots:
+            sums = correlate(csp, row, col, range(segs[0], min(segs[-1] + 2, NSEG)))
+            for r in segs:
+                re, im = sums[r]
+                if r + 1 < NSEG:
+                    re += lane_sign * sums[r + 1][0]
+                    im += lane_sign * sums[r + 1][1]
+                put(base + r, row, col, re)
+                put(base + r, row, SEG + col, im)
+
+    def inverse(rows):
+        return jnp.dot(abuf[rows], inv_v[...], preferred_element_type=F32).astype(BF16)
+
+    head, rest = pl.ds(0, SUB), pl.ds(SUB, (NSEG - 1) * SUB)
+    grads(range(1), 0)
+    lags(range(1), NSEG)
+    y_s[head] = inverse(head)
+    collect_first(y_s, y_r, 3)
+    l_s[head] = inverse(pl.ds(NSEG * SUB, SUB))
+    collect_first(l_s, l_r, 4)
+    grads(range(1, NSEG), 0)
+    y_s[rest] = inverse(rest)
     collect(y_s, y_r, 3)
-
-    lane_sign = sign[:, :128]
-
-    for row, col in spots:
-        lags = correlate(csp, row, col)
-        for r, (re, im) in enumerate(lags):
-            if r + 1 < NSEG:
-                re += lane_sign * lags[r + 1][0]
-                im += lane_sign * lags[r + 1][1]
-            put(r, row, col, re)
-            put(r, row, SEG + col, im)
-
-    l_s[...] = jnp.dot(abuf[...], inv_v[...], preferred_element_type=F32).astype(BF16)
+    lags(range(1, NSEG), 0)
+    l_s[rest] = inverse(rest)
     collect(l_s, l_r, 4)
 
     all_in(y_r, 3)
@@ -356,16 +378,16 @@
     all_in(l_r, 4)
     out_ref[pl.ds(LS, LS)] = l_r[...].astype(F32).T.astype(BF16)
 
-    def drain(part, i):
+    def drain(chunks, i):
+        rows = next(r for r in range(LS, 0, -16) if chunks * CHUNK % r == 0)
+        part = x_v.at[pl.ds(0, chunks * CHUNK // rows), pl.ds(0, rows)]
         pltpu.make_async_copy(part, part, ring_send.at[i]).wait()
 
-    drain(x_v.at[pl.ds(0, 9)], 0)
-    drain(x_v.at[pl.ds(0, 9), pl.ds(0, 2 * CHUNK)], 1)
+    flows = CHUNKS + len(ROWS_B)
+    drain(6 * flows, 0)
+    drain(NZ * N_A + len(ROWS_B), 1)
     for side in (0, 1):
-
-        @pl.when(goes_on[side])
-        def _():
-            drain(x_v.at[pl.ds(0, 3), pl.ds(0, 2 * CHUNK)], 2 + side)
+        pl.when(goes_on[side])(functools.partial(drain, flows, 2 + side))
 
     for which, block in enumerate((ct_s, tt_s, gt_s, y_s, l_s)):
         all_out(block, which)
@@ -400,7 +422,7 @@
             pltpu.VMEM((NSEG * SUB, 2 * SEG), F32),
             pltpu.VMEM((NSEG * SUB, 3 * SEG), F32),
             pltpu.VMEM((NSEG * SUB, 3 * SEG), F32),
-            pltpu.VMEM((NSEG * SUB, 2 * SEG), BF16),
+            pltpu.VMEM(((NSEG + 1) * SUB, 2 * SEG), BF16),
             pltpu.VMEM(local, BF16),
             pltpu.VMEM(local, BF16),
             pltpu.VMEM(turned, BF16),
@@ -408,8 +430,8 @@
             pltpu.SemaphoreType.DMA((4,)),
             pltpu.SemaphoreType.DMA,
             pltpu.SemaphoreType.DMA((4,)),
-            pltpu.SemaphoreType.DMA((NZ, 4)),
-            pltpu.SemaphoreType.DMA((NZ, 2)),
+            pltpu.SemaphoreType.DMA((NZ, CHUNKS)),
+            pltpu.SemaphoreType.DMA((NZ, CHUNKS - N_A)),
             pltpu.SemaphoreType.DMA((NZ,)),
             pltpu.SemaphoreType.DMA((5,)),
             pltpu.SemaphoreType.DMA((5,)),

time: 43.3 us -> 42.4 us (0.979)
  Pallas kernels: 41.7 us -> 40.8 us
    pallas_call x1, Pallas kernels: 41.7 us -> 40.8 us  [shards(): pl.pallas_call(kernel, out_shape=pltpu.VMEM((2 * LS, CH), BF16), in_specs...]
where the time goes in v5:
time: 42.4 us
  Pallas kernels  40.8 us (96%)
  other arithmetic  0.83 us (2%)
  between operations  0.67 us (2%)
    pallas_call x1, Pallas kernels, shards(): pl.pallas_call(kernel, out_shape=pltpu.VMEM((2 * LS, CH), BF16), in_specs...  40.8 us

profile of v5, /device:TPU:1, one launch (start us, length us, event | category | flops | bytes accessed | tf_op | source)
XLA Modules:
  0.0 42.4 jit_solution(7291502622685528315)
XLA Ops:
  0.6 0.0 copy-start.1
  0.6 0.0 copy-start
  0.7 40.8 %hyena_backward.1 = bf16[256,512]{1,0:T(8,128)(2,1)S(1)} custom-call(bf16[128,512]{1,0:T(8,128)(2,1)} %go_hbm.1, bf16[512,8192]{1,0:T(8,128)(2,1)} %w_hbm.1, bf16[128,512]{1,0:T(8,128)(2,1)} %q_hbm.1, bf16[128,512]{1,0:T(8,128)(2,1)} %key_hbm.1, bf16[128,512]{1,0:T(8,128)(2,1)} %val_hbm.1, bf16[128,512]{1,0:T(8,128)(2,1)} %taps_hbm.1, ...), custom_call_target="tpu_custom_call" | custom-call | tf_op jit(solution)/shard_map/hyena_backward/pallas_call | solution.py:403
  41.5 0.0 copy-done.1
  41.5 0.0 copy-done
  41.5 0.8 %convert_multiply_fusion.2 = (f32[128,512]{1,0:T(8,128)}, bf16[128,512]{1,0:T(8,128)(2,1)}, bf16[128,512]{1,0:T(8,128)(2,1)}) fusion(bf16[256,512]{1,0:T(8,128)(2,1)S(1)} %hyena_backward.1, bf16[128,512]{1,0:T(8,128)(2,1)S(1)} %copy-done, bf16[128,512]{1,0:T(8,128)(2,1)S(1)} %copy-done.1), kind=kLoop, calls=%fused_computation.4 | loop fusion | flops 589824 | bytes 1048576 | tf_op jit(solution)/shard_map/mul | solution.py:449
Async XLA Ops:
  0.6 40.9 %copy-start.1 = (bf16[128,512]{1,0:T(8,128)(2,1)S(1)}, bf16[128,512]{1,0:T(8,128)(2,1)}, u32[]{:S(2)}) copy-start(bf16[128,512]{1,0:T(8,128)(2,1)} %val_hbm.1) | copy-start | bytes 393220
  0.6 40.9 %copy-start = (bf16[128,512]{1,0:T(8,128)(2,1)S(1)}, bf16[128,512]{1,0:T(8,128)(2,1)}, u32[]{:S(2)}) copy-start(bf16[128,512]{1,0:T(8,128)(2,1)} %key_hbm.1) | copy-start | bytes 393220

commit v6 on v5

--- a/solution.py
+++ b/solution.py
@@ -197,15 +197,18 @@
     for row in ROWS_B:
         start_ring(0, row)
 
-    def scatter(block, recv, which):
+    def scatter(block, recv, which, only_dx=None):
         my_row = pl.ds(pl.multiple_of(pair_in_seq * SUB, SUB), SUB)
         my_col = pl.ds(pl.multiple_of(core * LS, LS), LS)
-        pltpu.make_async_copy(
-            block.at[pl.ds(pl.multiple_of(s * SUB, SUB), SUB)],
-            recv.at[my_row, my_col],
-            a2a_recv.at[which],
-        ).start()
+        if not only_dx:
+            pltpu.make_async_copy(
+                block.at[pl.ds(pl.multiple_of(s * SUB, SUB), SUB)],
+                recv.at[my_row, my_col],
+                a2a_recv.at[which],
+            ).start()
         for hop in HOPS:
+            if only_dx not in (None, hop[0]):
+                continue
             to = seq_of(hop)
             pltpu.make_async_remote_copy(
                 src_ref=block.at[pl.ds(pl.multiple_of(to * SUB, SUB), SUB)],
@@ -279,9 +282,6 @@
     mult_pair(2)
     arrived_across(0)
     mult(8)
-    ring_own(3)
-    ring_pair(2)
-
     def put3(ref, cos, sin):
         ref[:, pl.ds(0, SEG)] = cos
         ref[:, pl.ds(SEG, SEG)] = jnp.where(first, 0.0, sin)
@@ -291,9 +291,9 @@
     all_in(c_r, 0)
     spec = jnp.dot(c_r[...], fwd_v[...], preferred_element_type=F32)
     put3(csp, spec[:, :SEG], spec[:, SEG:])
-    mult_pair(3)
-    ring_own(4)
-    ring_pair(3)
+    ring_own(3)
+    ring_pair(2)
+
     all_in(t_r, 1)
     spec = jnp.dot(t_r[...], fwd_v[...], preferred_element_type=F32)
     before = jnp.concatenate([jnp.zeros((SUB, 2 * SEG), F32), spec[:-SUB]], 0)
@@ -302,17 +302,25 @@
         spec[:, :SEG] + sign * before[:, :SEG],
         spec[:, SEG:] + sign * before[:, SEG:],
     )
+    mult_pair(3)
+    ring_own(4)
+    ring_pair(3)
     inv_load.wait()
     mult(7)
     mult_pair(NZ + 1, True)
     mult_pair(NZ + 2, True)
+    mult_pair(NZ + 3, True)
     ring_pair(4)
-    mult_pair(NZ + 3, True)
     arrived_across(LAST)
-    mult(NZ + LAST)
-
-    gt_s[...] = (acc[...] * qt[...]).astype(BF16)
-    scatter(gt_s, g_r, 2)
+
+    for dx in (2, 1, 3, 0):
+        part = pl.ds(pl.multiple_of(lax.rem(x + dx, 4) * LS, LS), LS)
+        product = acc[part] + lax.dot_general(
+            w_v[NZ + LAST, part], x_v[NZ + LAST], (((1,), (1,)), ((), ())),
+            preferred_element_type=F32,
+        )
+        gt_s[part] = (product * qt[part]).astype(BF16)
+        scatter(gt_s, g_r, 2, dx)
     all_in(g_r, 2)
     gsp[...] = jnp.dot(g_r[...], fwd_v[...], preferred_element_type=F32)
 

time: 42.4 us -> 41.8 us (0.986)
  Pallas kernels: 40.8 us -> 40.2 us
    pallas_call x1, Pallas kernels: 40.8 us -> 40.2 us  [shards(): pl.pallas_call(kernel, out_shape=pltpu.VMEM((2 * LS, CH), BF16), in_specs...]
where the time goes in v6:
time: 41.8 us; the launch traced here: 41.7 us
  Pallas kernels  40.2 us (96%)
  other arithmetic  0.83 us (2%)
  between operations  0.67 us (2%)
    pallas_call x1, Pallas kernels, shards(): pl.pallas_call(kernel, out_shape=pltpu.VMEM((2 * LS, CH), BF16), in_specs...  40.2 us

profile of v6, /device:TPU:1, one launch (start us, length us, event | category | flops | bytes accessed | tf_op | source)
XLA Modules:
  0.0 41.7 jit_solution(15813965352503153603)
XLA Ops:
  0.6 0.0 copy-start.1
  0.6 0.0 copy-start
  0.7 40.2 %hyena_backward.1 = bf16[256,512]{1,0:T(8,128)(2,1)S(1)} custom-call(bf16[128,512]{1,0:T(8,128)(2,1)} %go_hbm.1, bf16[512,8192]{1,0:T(8,128)(2,1)} %w_hbm.1, bf16[128,512]{1,0:T(8,128)(2,1)} %q_hbm.1, bf16[128,512]{1,0:T(8,128)(2,1)} %key_hbm.1, bf16[128,512]{1,0:T(8,128)(2,1)} %val_hbm.1, bf16[128,512]{1,0:T(8,128)(2,1)} %taps_hbm.1, ...), custom_call_target="tpu_custom_call" | custom-call | tf_op jit(solution)/shard_map/hyena_backward/pallas_call | solution.py:411
  40.9 0.0 copy-done.1
  40.9 0.0 copy-done
  40.9 0.8 %convert_multiply_fusion.2 = (f32[128,512]{1,0:T(8,128)}, bf16[128,512]{1,0:T(8,128)(2,1)}, bf16[128,512]{1,0:T(8,128)(2,1)}) fusion(bf16[256,512]{1,0:T(8,128)(2,1)S(1)} %hyena_backward.1, bf16[128,512]{1,0:T(8,128)(2,1)S(1)} %copy-done, bf16[128,512]{1,0:T(8,128)(2,1)S(1)} %copy-done.1), kind=kLoop, calls=%fused_computation.4 | loop fusion | flops 589824 | bytes 1048576 | tf_op jit(solution)/shard_map/mul | solution.py:457
Async XLA Ops:
  0.6 40.3 %copy-start.1 = (bf16[128,512]{1,0:T(8,128)(2,1)S(1)}, bf16[128,512]{1,0:T(8,128)(2,1)}, u32[]{:S(2)}) copy-start(bf16[128,512]{1,0:T(8,128)(2,1)} %val_hbm.1) | copy-start | bytes 393220
  0.6 40.3 %copy-start = (bf16[128,512]{1,0:T(8,128)(2,1)S(1)}, bf16[128,512]{1,0:T(8,128)(2,1)}, u32[]{:S(2)}) copy-start(bf16[128,512]{1,0:T(8,128)(2,1)} %key_hbm.1) | copy-start | bytes 393220

commit v7 on v6

--- a/solution.py
+++ b/solution.py
@@ -381,11 +381,6 @@
     l_s[rest] = inverse(rest)
     collect(l_s, l_r, 4)
 
-    all_in(y_r, 3)
-    out_ref[pl.ds(0, LS)] = y_r[...].astype(F32).T.astype(BF16)
-    all_in(l_r, 4)
-    out_ref[pl.ds(LS, LS)] = l_r[...].astype(F32).T.astype(BF16)
-
     def drain(chunks, i):
         rows = next(r for r in range(LS, 0, -16) if chunks * CHUNK % r == 0)
         part = x_v.at[pl.ds(0, chunks * CHUNK // rows), pl.ds(0, rows)]
@@ -396,9 +391,15 @@
     drain(NZ * N_A + len(ROWS_B), 1)
     for side in (0, 1):
         pl.when(goes_on[side])(functools.partial(drain, flows, 2 + side))
-
-    for which, block in enumerate((ct_s, tt_s, gt_s, y_s, l_s)):
+    for which, block in enumerate((ct_s, tt_s, gt_s)):
         all_out(block, which)
+
+    all_in(y_r, 3)
+    out_ref[pl.ds(0, LS)] = y_r[...].astype(F32).T.astype(BF16)
+    all_out(y_s, 3)
+    all_in(l_r, 4)
+    out_ref[pl.ds(LS, LS)] = l_r[...].astype(F32).T.astype(BF16)
+    all_out(l_s, 4)
 
 
 def shards(grad_out, out_weight, query_gate, key_branch, value_branch, filter_taps):

time: 41.8 us -> 41.8 us (level)
  no operation moved by 1% of the time
where the time goes in v7:
time: 41.8 us; the launch traced here: 41.7 us
  Pallas kernels  40.2 us (96%)
  other arithmetic  0.83 us (2%)
  between operations  0.67 us (2%)
    pallas_call x1, Pallas kernels, shards(): pl.pallas_call(kernel, out_shape=pltpu.VMEM((2 * LS, CH), BF16), in_specs...  40.2 us

profile of v7, /device:TPU:1, one launch (start us, length us, event | category | flops | bytes accessed | tf_op | source)
XLA Modules:
  0.0 41.7 jit_solution(7782986047821013487)
XLA Ops:
  0.6 0.0 copy-start.1
  0.6 0.0 copy-start
  0.7 40.2 %hyena_backward.1 = bf16[256,512]{1,0:T(8,128)(2,1)S(1)} custom-call(bf16[128,512]{1,0:T(8,128)(2,1)} %go_hbm.1, bf16[512,8192]{1,0:T(8,128)(2,1)} %w_hbm.1, bf16[128,512]{1,0:T(8,128)(2,1)} %q_hbm.1, bf16[128,512]{1,0:T(8,128)(2,1)} %key_hbm.1, bf16[128,512]{1,0:T(8,128)(2,1)} %val_hbm.1, bf16[128,512]{1,0:T(8,128)(2,1)} %taps_hbm.1, ...), custom_call_target="tpu_custom_call" | custom-call | tf_op jit(solution)/shard_map/hyena_backward/pallas_call | solution.py:412
  40.9 0.0 copy-done.1
  40.9 0.0 copy-done
  40.9 0.8 %convert_multiply_fusion.2 = (f32[128,512]{1,0:T(8,128)}, bf16[128,512]{1,0:T(8,128)(2,1)}, bf16[128,512]{1,0:T(8,128)(2,1)}) fusion(bf16[256,512]{1,0:T(8,128)(2,1)S(1)} %hyena_backward.1, bf16[128,512]{1,0:T(8,128)(2,1)S(1)} %copy-done, bf16[128,512]{1,0:T(8,128)(2,1)S(1)} %copy-done.1), kind=kLoop, calls=%fused_computation.4 | loop fusion | flops 589824 | bytes 1048576 | tf_op jit(solution)/shard_map/mul | solution.py:458
Async XLA Ops:
  0.6 40.3 %copy-start.1 = (bf16[128,512]{1,0:T(8,128)(2,1)S(1)}, bf16[128,512]{1,0:T(8,128)(2,1)}, u32[]{:S(2)}) copy-start(bf16[128,512]{1,0:T(8,128)(2,1)} %val_hbm.1) | copy-start | bytes 393220
  0.6 40.3 %copy-start = (bf16[128,512]{1,0:T(8,128)(2,1)S(1)}, bf16[128,512]{1,0:T(8,128)(2,1)}, u32[]{:S(2)}) copy-start(bf16[128,512]{1,0:T(8,128)(2,1)} %key_hbm.1) | copy-start | bytes 393220
